TPU v7x, 256 devices: a whole 4x4x8 slice. The times are simulated.
256 devices in a mesh: req: 32 (over z, x_lo, core), tp: 8 (over x_hi, y).
Axes of the slice: x: 4 (x_hi: 2, x_lo: 2; x = x_hi * 2 + x_lo), y: 4, z: 8, core: 2. Of those that a mesh axis runs over, the one named last changes fastest.
Arguments:
- suffix_query: bfloat16 [8192, 5120], P('req', 'tp')
- suffix_key: bfloat16 [8192, 1024], P('req', 'tp')
- suffix_value: bfloat16 [8192, 1024], P('req', 'tp'), may hold values from -6 to 6
- prefix_key: bfloat16 [32, 1024, 1024], P('req', None, 'tp')
- prefix_value: bfloat16 [32, 1024, 1024], P('req', None, 'tp'), may hold values from -6 to 6
- residual: bfloat16 [8192, 5120], P('req'), may hold values from -6 to 6
- out_weight: bfloat16 [5120, 5120], P('tp'), may hold values from -0.15625 to 0.15625
- norm_gain: bfloat16 [5120], P('tp'), may hold values from 0.099609375 to 1.8984375
- lengths: int32 [32], replicated, may hold values from 1 to 256, 4915 in all
- request_slot: int32 [32], replicated, may hold values from 0 to 31, each once
- prefix_owner: int32 [32], replicated, may hold values from 0 to 31, each once
- request_group: int32 [32, 1], replicated, may hold values from 0 to 3
Outputs:
- hidden: bfloat16 [8192, 5120], P('req', 'tp')
- normed: bfloat16 [8192, 5120], P('req', 'tp')
- cache_key: bfloat16 [8192, 1024], P('req', 'tp')
Inputs may be any that keep to these rules, and one draw needn't show every extreme that they name: `request_slot`: a permutation. `prefix_owner`: a permutation. `request_group`: every group has one request or more. `lengths`: some request has all 256 slots live.
All inputs are finite; a program needn't handle non-finite values.
Results may differ from a plain program's by a relative error of at most 0.0067.
Values may be sent and summed in bfloat16 or wider, within the bound.
No kernel may reach another device: no remote copies, remote signals or barrier semaphores. Data moves between devices by JAX's collectives and lax.ppermute only.
A program may use at most 128 MiB of HBM per device.

v0:
```python
import jax
import jax.numpy as jnp
from jax import lax
from jax.experimental import pallas as pl
from jax.experimental.pallas import tpu as pltpu
from jax.sharding import PartitionSpec as P


HD = 128
GROUPS = 4
PLANE = 4
TILE = 128
THETA = 1000000.0
NEGATIVE = -1e30
EPSILON = 1e-06
LOG2E = 1.4426950408889634


SMEM = pltpu.SMEM
VMEM = pltpu.VMEM


def full(space=VMEM):
    return pl.BlockSpec(memory_space=space)


def params(limit=40):
    return pltpu.CompilerParams(vmem_limit_bytes=limit * 1024 * 1024)


RATE = HD ** (-0.5) * LOG2E
NT = (((1,), (1,)), ((), ()))


def turn(x, cosines, sines):
    return x * cosines + pltpu.roll(x, HD // 2, 1) * sines


def turn_tiles(q_in, q_ref, at, cosines, sines):
    for j in range(q_in.shape[0] // TILE):
        rows = slice(j * TILE, (j + 1) * TILE)
        for h in range(q_ref.shape[1]):
            x = q_in[rows, h * HD : (h + 1) * HD].astype(jnp.float32)
            q_ref[at + j, h] = turn(x, cosines[rows], sines[rows]).astype(jnp.bfloat16)


def own_kernel(meta, q_in, k_in, v_in, cos_in, sin_in, q_out, key_out, acc_ref, max_ref, sum_ref):
    tiles, heads = q_out.shape[:2]
    slots = k_in.shape[0]
    length = meta[0]
    cosines = cos_in[...]
    sines = sin_in[...]
    turn_tiles(q_in, q_out, 0, cosines, sines)
    turned = turn(k_in[...].astype(jnp.float32), cosines, sines)
    place = lax.broadcasted_iota(jnp.int32, turned.shape, 0)
    key_out[...] = jnp.where(place < length, turned, 0.0).astype(jnp.bfloat16)
    max_ref[...] = jnp.zeros_like(max_ref)
    sum_ref[...] = jnp.ones_like(sum_ref)
    k = key_out[...]
    v = v_in[...].T
    u = lax.broadcasted_iota(jnp.int32, (slots, TILE), 0)
    t = lax.broadcasted_iota(jnp.int32, (slots, TILE), 1)
    for j in range(tiles):
        visible = (u <= t + j * TILE) & (u < length)
        for h in range(heads):
            scores = lax.dot_general(k, q_out[j, h], NT, preferred_element_type=jnp.float32)
            scores = jnp.where(visible, scores, NEGATIVE)
            top = jnp.max(scores, axis=0, keepdims=True)
            weights = jnp.exp2((scores - top) * RATE)
            max_ref[j, h : h + 1] = top
            sum_ref[j, h : h + 1] = jnp.sum(weights, axis=0, keepdims=True)
            acc_ref[j, h] = jnp.dot(v, weights.astype(jnp.bfloat16), preferred_element_type=jnp.float32)


def visit(meta, base, count, q_ref, kv_ref, vt_ref, s_ref, p_ref, top_ref, keep_ref, acc_ref, max_ref, sum_ref, items):
    heads = q_ref.shape[1]
    spare = q_ref.shape[0] - 1
    tiles = spare // PLANE
    part = kv_ref.shape[2]
    for e in range(count):
        vt_ref[e, :HD] = kv_ref[e, 1].T
        vt_ref[e, HD:] = jnp.ones((16, part), jnp.bfloat16)
    n = jnp.int32(0)
    for e in range(count):
        for i in range(PLANE):
            for j in range(tiles):
                live = (meta[2 * PLANE + (base + e) * PLANE + i] == 1) & (j < meta[PLANE + i])

                @pl.when(live)
                def _(n=n, e=e, i=i, j=j):
                    items[n, 0] = e
                    items[n, 1] = i * tiles + j

                n = n + live.astype(jnp.int32)
    for x in range(4):
        items[n + x, 0] = 0
        items[n + x, 1] = spare

    def score(step, slot):
        k = kv_ref[items[step, 0], 0]
        at = items[step, 1]
        for h in range(heads):
            scores = lax.dot_general(k, q_ref[at, h], NT, preferred_element_type=jnp.float32)
            s_ref[slot, h] = scores
            top_ref[slot, h : h + 1] = jnp.max(scores, axis=0, keepdims=True)

    def weigh(step, slot):
        at = items[step, 1]
        old = max_ref[at]
        new = jnp.maximum(old, top_ref[slot])
        max_ref[at] = new
        keep_ref[slot] = jnp.exp2((old - new) * RATE)
        for h in range(heads):
            p_ref[slot, h] = jnp.exp2((s_ref[slot, h] - new[h : h + 1]) * RATE).astype(jnp.bfloat16)

    def gather(step, slot):
        v = vt_ref[items[step, 0]]
        at = items[step, 1]
        keep = keep_ref[slot]
        for h in range(heads):
            mixed = jnp.dot(v, p_ref[slot, h], preferred_element_type=jnp.float32)
            acc_ref[at, h] = acc_ref[at, h] * keep[h : h + 1] + mixed[:HD]
            sum_ref[at, h : h + 1] = sum_ref[at, h : h + 1] * keep[h : h + 1] + mixed[HD : HD + 1]

    @pl.when(n > 0)
    def _():
        score(0, 0)
        score(1, 1)
        weigh(0, 0)

        def body(t, carry):
            for x in range(2):
                step = 2 * t + x
                score_slot = x
                gather(step, x)
                weigh(step + 1, 1 - x)
                score(step + 2, score_slot)
            return carry

        lax.fori_loop(0, (n + 1) // 2, body, 0)


def fetch(pairs, sems):
    copies = [
        pltpu.make_async_copy(source, target, sems.at[n])
        for n, (source, target) in enumerate(pairs)
    ]
    for copy in copies:
        copy.start()
    return copies


def make_first(base, count):
    def kernel(meta, q_own, acc_own, max_own, sum_own, q1, q2, q3, cos_in, sin_in, *rest):
        kv_in = rest[:count]
        q_ref, acc_ref, max_ref, sum_ref, sems, kv_ref, vt_ref, s_ref, p_ref, top_ref, keep_ref, items = rest[count:]
        copies = fetch([(kv, kv_ref.at[e]) for e, kv in enumerate(kv_in)], sems)
        tiles = q_own.shape[0]
        acc_ref[tiles:] = jnp.zeros_like(acc_ref[tiles:])
        max_ref[tiles:] = jnp.full_like(max_ref[tiles:], NEGATIVE)
        sum_ref[tiles:] = jnp.zeros_like(sum_ref[tiles:])
        top_ref[...] = jnp.zeros_like(top_ref)
        q_ref[:tiles] = q_own[...]
        q_ref[PLANE * tiles] = q_own[0]
        acc_ref[:tiles] = acc_own[...]
        max_ref[:tiles] = max_own[...]
        sum_ref[:tiles] = sum_own[...]
        cosines = cos_in[...]
        sines = sin_in[...]
        for i, q_in in enumerate((q1, q2, q3)):
            turn_tiles(q_in, q_ref, (i + 1) * tiles, cosines, sines)
        for copy in copies:
            copy.wait()
        visit(meta, base, count, q_ref, kv_ref, vt_ref, s_ref, p_ref, top_ref, keep_ref, acc_ref, max_ref, sum_ref, items)

    return kernel


def make_middle(base, count):
    def kernel(meta, q_ref, acc_in, max_in, sum_in, *rest):
        kv_in = rest[:count]
        acc_ref, max_ref, sum_ref, sems, kv_ref, vt_ref, s_ref, p_ref, top_ref, keep_ref, items = rest[count:]
        pairs = [(kv, kv_ref.at[e]) for e, kv in enumerate(kv_in)]
        copies = fetch(pairs + [(acc_in, acc_ref)], sems)
        max_ref[...] = max_in[...]
        sum_ref[...] = sum_in[...]
        top_ref[...] = jnp.zeros_like(top_ref)
        for copy in copies:
            copy.wait()
        visit(meta, base, count, q_ref, kv_ref, vt_ref, s_ref, p_ref, top_ref, keep_ref, acc_ref, max_ref, sum_ref, items)

    return kernel


def split(x):
    high = x.astype(jnp.bfloat16)
    left = x - high.astype(jnp.float32)
    middle = left.astype(jnp.bfloat16)
    low = (left - middle.astype(jnp.float32)).astype(jnp.bfloat16)
    return high, middle, low


def make_last(base, count):
    def kernel(meta, q_ref, acc_in, max_in, sum_in, *rest):
        kv_in = rest[:count]
        acc_own, max_own, sum_own, o1, o2, o3 = rest[count : count + 6]
        acc_ref, max_ref, sum_ref, sems, kv_ref, vt_ref, s_ref, p_ref, top_ref, keep_ref, items = rest[count + 6 :]
        pairs = [(kv, kv_ref.at[e]) for e, kv in enumerate(kv_in)]
        copies = fetch(pairs + [(acc_in, acc_ref)], sems)
        max_ref[...] = max_in[...]
        sum_ref[...] = sum_in[...]
        top_ref[...] = jnp.zeros_like(top_ref)
        for copy in copies:
            copy.wait()
        visit(meta, base, count, q_ref, kv_ref, vt_ref, s_ref, p_ref, top_ref, keep_ref, acc_ref, max_ref, sum_ref, items)
        tiles, heads = acc_own.shape[:2]
        acc_own[...] = acc_ref[:tiles]
        max_own[...] = max_ref[:tiles]
        sum_own[...] = sum_ref[:tiles]
        for i, out in enumerate((o1, o2, o3)):
            first = (i + 1) * tiles
            for j in range(tiles):
                total = sum_ref[first + j]
                inverse = jnp.where(total > 0, 1.0 / jnp.where(total > 0, total, 1.0), 0.0)
                for h in range(heads):
                    at = (j * heads + h) * HD
                    out[at : at + HD] = (acc_ref[first + j, h] * inverse[h : h + 1]).astype(jnp.bfloat16)
            at = tiles * heads * HD
            for stats in (max_ref, sum_ref):
                flat = jnp.concatenate([stats[first + j] for j in range(tiles)], axis=0)
                for piece in split(flat):
                    out[at : at + 8 * tiles] = piece
                    at = at + 8 * tiles

    return kernel


def combine_kernel(meta, where, acc_own, max_own, sum_own, o1, o2, o3, weight_in, *rest):
    ways = (len(rest) - 3)
    outs = rest[:ways]
    attn_ref, weight_ref, sems = rest[ways:]
    columns = weight_ref.shape[2]
    copies = []
    for k in range(ways):
        at = pl.multiple_of((where[0] ^ k) * columns, HD)
        copies.append(
            pltpu.make_async_copy(
                weight_in.at[:, pl.ds(at, columns)], weight_ref.at[k], sems.at[k]
            )
        )
    for copy in copies[1:] + copies[:1]:
        copy.start()
    tiles, heads = acc_own.shape[:2]
    rows = 8 * tiles
    maxima = [jnp.concatenate([max_own[j] for j in range(tiles)], axis=0)]
    sums = [jnp.concatenate([sum_own[j] for j in range(tiles)], axis=0)]
    for part in (o1, o2, o3):
        at = tiles * heads * HD
        found = []
        for _ in range(2):
            pieces = [
                part[at + n * rows : at + (n + 1) * rows].astype(jnp.float32) for n in range(3)
            ]
            found.append(pieces[0] + pieces[1] + pieces[2])
            at = at + 3 * rows
        maxima.append(found[0])
        sums.append(found[1])
    top = jnp.maximum(jnp.maximum(maxima[0], maxima[1]), jnp.maximum(maxima[2], maxima[3]))
    factor = [jnp.exp2((m - top) * RATE) for m in maxima]
    mass = [f * s for f, s in zip(factor, sums)]
    inverse = 1.0 / (mass[0] + mass[1] + mass[2] + mass[3])
    lane = lax.broadcasted_iota(jnp.int32, (HD, TILE), 1)
    shares = [factor[0] * inverse] + [m * inverse for m in mass[1:]]
    for j in range(tiles):
        live = lane + j * TILE < meta[0]
        for h in range(heads):
            r = j * 8 + h
            value = acc_own[j, h] * shares[0][r : r + 1]
            for w, part in zip(shares[1:], (o1, o2, o3)):
                at = (j * heads + h) * HD
                value = value + w[r : r + 1] * part[at : at + HD].astype(jnp.float32)
            value = jnp.transpose(jnp.where(live, value, 0.0))
            attn_ref[j * TILE : (j + 1) * TILE, h * HD : (h + 1) * HD] = value.astype(jnp.bfloat16)
    for k in list(range(1, ways)) + [0]:
        copies[k].wait()
        outs[k][...] = jnp.dot(
            attn_ref[...], weight_ref[k], preferred_element_type=jnp.float32
        ).astype(outs[k].dtype)


def cost(blocks, bytes_accessed):
    pairs = blocks * 1280 * 512
    return pl.CostEstimate(
        flops=4 * pairs * HD, bytes_accessed=bytes_accessed, transcendentals=pairs
    )


def shards(
    suffix_query,
    suffix_key,
    suffix_value,
    prefix_key,
    prefix_value,
    residual,
    out_weight,
    norm_gain,
    lengths,
    request_slot,
    prefix_owner,
    request_group,
):
    slots = suffix_query.shape[0]
    heads = suffix_query.shape[1] // HD
    devices = lax.axis_size("req")
    planes = devices // PLANE
    place = lax.axis_index("req")
    tensor = lax.axis_index("tp")
    ways = lax.axis_size("tp")
    per_group = devices // GROUPS
    block = prefix_key.shape[1]
    part = block // 2
    prefix_length = block * per_group
    bf16 = jnp.bfloat16
    f32 = jnp.float32

    def beside(k):
        return [(i, i ^ k) for i in range(devices)]

    up_pairs = [(i, (i + PLANE) % devices) for i in range(devices)]
    down_pairs = [(i, (i - PLANE) % devices) for i in range(devices)]

    core = place % 2
    both = jnp.concatenate([prefix_key, prefix_value], axis=0)
    mine = lax.dynamic_slice_in_dim(both, core * part, part, 1)
    theirs = lax.dynamic_slice_in_dim(both, (1 - core) * part, part, 1)
    lanes = [mine, lax.ppermute(theirs, "req", beside(1))]
    queries = [lax.ppermute(suffix_query, "req", beside(k)) for k in range(1, PLANE)]

    entries = {(0, 0): lanes[0], (0, 1): lanes[1]}
    half_way = planes // 2
    for lane in range(2):
        moving_up = lanes[lane]
        moving_down = lanes[lane]
        for step in range(1, half_way):
            moving_up = lax.ppermute(moving_up, "req", up_pairs)
            moving_down = lax.ppermute(moving_down, "req", down_pairs)
            entries[(-step, lane)] = moving_up
            entries[(step, lane)] = moving_down
        if lane == 0:
            entries[(-half_way, 0)] = lax.ppermute(moving_up, "req", up_pairs)
        else:
            entries[(half_way, 1)] = lax.ppermute(moving_down, "req", down_pairs)

    batches = [
        [(0, 0), (0, 1), (-1, 0), (1, 0), (-1, 1), (1, 1)],
        [(-2, 0), (2, 0), (-2, 1), (2, 1)],
        [(-3, 0), (3, 0), (-3, 1), (3, 1)],
        [(-half_way, 0), (half_way, 1)],
    ]
    order = [key for batch in batches for key in batch]

    numbers = jnp.arange(devices, dtype=jnp.int32)
    owner_match = prefix_owner[None, :] == numbers[:, None]
    holder_group = jnp.sum(jnp.where(owner_match, numbers[None, :], 0), axis=1) // per_group
    slot_match = request_slot[:, None] == numbers[None, :]
    asker_group = jnp.sum(jnp.where(slot_match, request_group[:, 0][None, :], 0), axis=1)
    asker_length = jnp.sum(jnp.where(slot_match, lengths[None, :], 0), axis=1)
    nearby = place ^ jnp.arange(PLANE, dtype=jnp.int32)
    near = nearby[:, None] == numbers[None, :]
    near_group = jnp.sum(jnp.where(near, asker_group[None, :], 0), axis=1)
    near_length = jnp.sum(jnp.where(near, asker_length[None, :], 0), axis=1)
    shift = jnp.array([key[0] for key in order], jnp.int32)
    twist = jnp.array([key[1] for key in order], jnp.int32)
    source = ((place // PLANE + shift) % planes) * PLANE + ((place % PLANE) ^ twist)
    from_there = source[:, None] == numbers[None, :]
    source_group = jnp.sum(jnp.where(from_there, holder_group[None, :], 0), axis=1)
    match = (source_group[:, None] == near_group[None, :]).astype(jnp.int32)
    tiles = (near_length + TILE - 1) // TILE
    meta = jnp.concatenate([near_length, tiles, match.reshape(-1)])

    half_dim = HD // 2
    positions = (prefix_length + jnp.arange(slots)).astype(f32)
    frequency = THETA ** (-(jnp.arange(half_dim).astype(f32) * 2.0 / HD))
    angles = positions[:, None] * frequency[None, :]
    cosines = jnp.cos(angles)
    sines = jnp.sin(angles)
    cosines = jnp.concatenate([cosines, cosines], axis=1)
    sines = jnp.concatenate([-sines, sines], axis=1)

    tiles_each = slots // TILE
    shape = jax.ShapeDtypeStruct
    q_own, cache_key, acc_own, max_own, sum_own = pl.pallas_call(
        own_kernel,
        out_shape=(
            shape((tiles_each, heads, TILE, HD), bf16),
            shape((slots, HD), bf16),
            shape((tiles_each, heads, HD, TILE), f32),
            shape((tiles_each, 8, TILE), f32),
            shape((tiles_each, 8, TILE), f32),
        ),
        in_specs=[full(SMEM)] + [full()] * 5,
        out_specs=(full(),) * 5,
        cost_estimate=cost(1, 3 << 20),
        compiler_params=params(),
        name="own",
    )(meta, suffix_query, suffix_key, suffix_value, cosines, sines)

    every = PLANE * tiles_each + 1
    state_shapes = (
        shape((every, heads, HD, TILE), f32),
        shape((every, 8, TILE), f32),
        shape((every, 8, TILE), f32),
    )

    def work(count):
        return [
            pltpu.SemaphoreType.DMA((count + 1,)),
            pltpu.VMEM((count, 2, part, HD), bf16),
            pltpu.VMEM((count, HD + 16, part), bf16),
            pltpu.VMEM((2, heads, part, TILE), f32),
            pltpu.VMEM((2, heads, part, TILE), bf16),
            pltpu.VMEM((2, 8, TILE), f32),
            pltpu.VMEM((2, 8, TILE), f32),
            pltpu.SMEM((count * PLANE * tiles_each + 4, 2), jnp.int32),
        ]

    base = 0
    parts = [entries[key] for key in batches[0]]
    q_all, *state = pl.pallas_call(
        make_first(base, len(parts)),
        out_shape=(shape((every, heads, TILE, HD), bf16),) + state_shapes,
        in_specs=[full(SMEM)] + [full()] * 9 + [full(pl.ANY)] * len(parts),
        out_specs=(full(),) * 4,
        scratch_shapes=work(len(parts)),
        cost_estimate=cost(len(parts), 8 << 20),
        compiler_params=params(),
        name="first",
    )(meta, q_own, acc_own, max_own, sum_own, *queries, cosines, sines, *parts)
    base += len(parts)
    for batch in batches[1:-1]:
        parts = [entries[key] for key in batch]
        state = pl.pallas_call(
            make_middle(base, len(parts)),
            out_shape=state_shapes,
            in_specs=[full(SMEM), full(), full(pl.ANY), full(), full()] + [full(pl.ANY)] * len(parts),
            out_specs=(full(),) * 3,
            scratch_shapes=work(len(parts)),
            cost_estimate=cost(len(parts), 8 << 20),
            compiler_params=params(),
            name="middle",
        )(meta, q_all, *state, *parts)
        base += len(parts)
    parts = [entries[key] for key in batches[-1]]
    packed = heads * slots + 2 * 3 * 8 * tiles_each
    last = pl.pallas_call(
        make_last(base, len(parts)),
        out_shape=(
            shape((tiles_each, heads, HD, TILE), f32),
            shape((tiles_each, 8, TILE), f32),
            shape((tiles_each, 8, TILE), f32),
        )
        + (shape((packed, HD), bf16),) * (PLANE - 1),
        in_specs=[full(SMEM), full(), full(pl.ANY), full(), full()] + [full(pl.ANY)] * len(parts),
        out_specs=(full(),) * (PLANE + 2),
        scratch_shapes=[
            pltpu.VMEM((every, heads, HD, TILE), f32),
            pltpu.VMEM((every, 8, TILE), f32),
            pltpu.VMEM((every, 8, TILE), f32),
        ]
        + work(len(parts)),
        cost_estimate=cost(len(parts), 8 << 20),
        compiler_params=params(),
        name="last",
    )(meta, q_all, *state, *parts)
    returned = [
        lax.ppermute(out, "req", beside(k)) for k, out in zip(range(1, PLANE), last[3:])
    ]
    width = residual.shape[1]
    columns = width // ways
    where = tensor.astype(jnp.int32).reshape(1)
    pieces = pl.pallas_call(
        combine_kernel,
        out_shape=tuple(shape((slots, columns), bf16 if k else f32) for k in range(ways)),
        in_specs=[full(SMEM)] * 2 + [full()] * 6 + [full(pl.ANY)],
        out_specs=(full(),) * ways,
        scratch_shapes=[
            pltpu.VMEM((slots, heads * HD), bf16),
            pltpu.VMEM((ways, heads * HD, columns), bf16),
            pltpu.SemaphoreType.DMA((ways,)),
        ],
        cost_estimate=pl.CostEstimate(
            flops=2 * slots * heads * HD * width, bytes_accessed=12 << 20, transcendentals=0
        ),
        compiler_params=params(60),
        name="combine",
    )(meta, where, *last[:3], *returned, out_weight)
    sent = [
        lax.ppermute(pieces[k], "tp", [(i, i ^ k) for i in range(ways)])
        for k in range(1, ways)
    ]
    shared = pieces[0]
    for piece in sent:
        shared = shared + piece.astype(f32)
    own_residual = lax.dynamic_slice_in_dim(residual, tensor * columns, columns, 1)
    hidden = (own_residual.astype(f32) + shared).astype(bf16)
    widened = hidden.astype(f32)
    squares = jnp.sum(widened * widened, axis=1).reshape(slots // HD, HD)
    squares = jnp.pad(squares, ((0, 8 - slots // HD), (0, 0)))
    spread = lax.all_to_all(jnp.broadcast_to(squares[None], (ways, 8, HD)), "tp", 0, 0)
    row_squares = jnp.sum(spread, axis=0)[: slots // HD].reshape(slots)
    scale_rows = lax.rsqrt(row_squares / width + EPSILON)
    normed = (widened * scale_rows[:, None] * norm_gain.astype(f32)[None, :]).astype(bf16)
    return (hidden, normed, cache_key)


def solution(mesh):
    return jax.shard_map(
        shards,
        mesh=mesh,
        in_specs=(
            P("req", "tp"),
            P("req", "tp"),
            P("req", "tp"),
            P("req", None, "tp"),
            P("req", None, "tp"),
            P("req", None),
            P("tp", None),
            P("tp"),
            P(),
            P(),
            P(),
            P(),
        ),
        out_specs=(P("req", "tp"), P("req", "tp"), P("req", "tp")),
        check_vma=False,
    )
```

profile of v0, /device:TPU:2, one launch (start us, length us, event | category | flops | bytes accessed | tf_op | source)
XLA Modules:
  0.0 163.4 jit_solution(16468543581724271364)
XLA Ops:
  0.6 0.0 copy-start.4
  0.7 1.0 constant_dynamic-update-slice_fusion.1
  1.7 1.0 constant_dynamic-update-slice_fusion
  2.8 2.0 %collective-permute-start.4 = (bf16[2,512,128]{2,1,0:T(8,128)(2,1)S(1)}, bf16[2,512,128]{2,1,0:T(8,128)(2,1)S(1)}, u32[]{:S(2)}, u32[]{:S(2)}) collective-permute-start(bf16[2,512,128]{2,1,0:T(8,128)(2,1)S(1)} %get-tuple-element.68.rest_0_), channel_id=1, source_target_pairs={{0,32},{8,40},{16,48},{24,56},{32,64},{40,72},{48,80},{56,88},{64,... | collective-permute-start | bytes 786440 | tf_op jit(solution)/shard_map/ppermute | solution.py:345
  4.7 4.0 %collective-permute-start.5 = (bf16[2,512,128]{2,1,0:T(8,128)(2,1)S(1)}, bf16[2,512,128]{2,1,0:T(8,128)(2,1)S(1)}, u32[]{:S(2)}, u32[]{:S(2)}) collective-permute-start(bf16[2,512,128]{2,1,0:T(8,128)(2,1)S(1)} %get-tuple-element.68.rest_0_), channel_id=1, source_target_pairs={{0,224},{8,232},{16,240},{24,248},{32,0},{40,8},{48,16},{56,24},{6... | collective-permute-start | bytes 786440 | tf_op jit(solution)/shard_map/ppermute | solution.py:346
  8.8 0.5 collective-permute-start.1
  9.3 0.2 collective-permute-start.3
  9.5 0.8 select_reduce_fusion.1
  10.3 0.9 select_reduce_fusion.2
  11.2 0.7 fusion.6
  11.9 1.3 fusion.3
  13.2 1.9 %collective-permute-start.7 = (bf16[2,512,128]{2,1,0:T(8,128)(2,1)S(1)}, bf16[2,512,128]{2,1,0:T(8,128)(2,1)S(1)}, u32[]{:S(2)}, u32[]{:S(2)}) collective-permute-start(bf16[2,512,128]{2,1,0:T(8,128)(2,1)S(1)} %collective-permute-done.3.rest_1_), channel_id=1, source_target_pairs={{0,224},{8,232},{16,240},{24,248},{32,0},{40,8},{48,16},{56,24},{6... | collective-permute-start | bytes 786440 | tf_op jit(solution)/shard_map/ppermute | solution.py:346
  15.1 0.2 select_reduce_fusion.5
  15.3 0.2 select_reduce_fusion.3
  15.5 0.2 collective-permute-start.6
  15.7 0.1 collective-permute-start.8
  15.8 5.9 %collective-permute-done.7.rest_5_ = bf16[2,512,128]{2,1,0:T(8,128)(2,1)S(1)} collective-permute-done((bf16[2,512,128]{2,1,0:T(8,128)(2,1)S(1)}, bf16[2,512,128]{2,1,0:T(8,128)(2,1)S(1)}, u32[]{:S(2)}, u32[]{:S(2)}) %collective-permute-start.7) | collective-permute-done | bytes 262176 | tf_op jit(solution)/shard_map/ppermute | solution.py:346
  21.7 3.1 %collective-permute-start.11 = (bf16[2,512,128]{2,1,0:T(8,128)(2,1)S(1)}, bf16[2,512,128]{2,1,0:T(8,128)(2,1)S(1)}, u32[]{:S(2)}, u32[]{:S(2)}) collective-permute-start(bf16[2,512,128]{2,1,0:T(8,128)(2,1)S(1)} %collective-permute-done.7.rest_5_), channel_id=1, source_target_pairs={{0,224},{8,232},{16,240},{24,248},{32,0},{40,8},{48,16},{56,24},{6... | collective-permute-start | bytes 786440 | tf_op jit(solution)/shard_map/ppermute | solution.py:346
  24.8 0.1 compare_convert_fusion
  24.9 0.3 collective-permute-start.2
  25.2 0.5 and_select_fusion.2
  25.7 0.1 reshape.77
  25.8 0.4 collective-permute-start.9
  26.2 1.7 %collective-permute-start.10 = (bf16[2,512,128]{2,1,0:T(8,128)(2,1)S(1)}, bf16[2,512,128]{2,1,0:T(8,128)(2,1)S(1)}, u32[]{:S(2)}, u32[]{:S(2)}) collective-permute-start(bf16[2,512,128]{2,1,0:T(8,128)(2,1)S(1)} %collective-permute-done.6.rest_4_), channel_id=1, source_target_pairs={{0,32},{8,40},{16,48},{24,56},{32,64},{40,72},{48,80},{56,88},{64,... | collective-permute-start | bytes 786440 | tf_op jit(solution)/shard_map/ppermute | solution.py:345
  27.9 2.7 %collective-permute-done.8.rest_0_ = bf16[2,512,128]{2,1,0:T(8,128)(2,1)S(1)} collective-permute-done((bf16[2,512,128]{2,1,0:T(8,128)(2,1)S(1)}, bf16[2,512,128]{2,1,0:T(8,128)(2,1)S(1)}, u32[]{:S(2)}, u32[]{:S(2)}) %collective-permute-start.8) | collective-permute-done | bytes 262176 | tf_op jit(solution)/shard_map/ppermute | solution.py:345
  30.6 0.9 collective-permute-done.11.rest_3_
  31.5 3.7 %collective-permute-start.15 = (bf16[2,512,128]{2,1,0:T(8,128)(2,1)S(1)}, bf16[2,512,128]{2,1,0:T(8,128)(2,1)S(1)}, u32[]{:S(2)}, u32[]{:S(2)}) collective-permute-start(bf16[2,512,128]{2,1,0:T(8,128)(2,1)S(1)} %collective-permute-done.11.rest_3_), channel_id=1, source_target_pairs={{0,224},{8,232},{16,240},{24,248},{32,0},{40,8},{48,16},{56,24},{6... | collective-permute-start | bytes 786440 | tf_op jit(solution)/shard_map/ppermute | solution.py:346
  35.2 0.7 pad_add_fusion.meta
  36.0 1.2 pad_maximum_fusion
  37.2 1.5 own.1
  38.7 2.1 %collective-permute-start.13 = (bf16[2,512,128]{2,1,0:T(8,128)(2,1)S(1)}, bf16[2,512,128]{2,1,0:T(8,128)(2,1)S(1)}, u32[]{:S(2)}, u32[]{:S(2)}) collective-permute-start(bf16[2,512,128]{2,1,0:T(8,128)(2,1)S(1)} %collective-permute-done.9.rest_1_), channel_id=1, source_target_pairs={{0,224},{8,232},{16,240},{24,248},{32,0},{40,8},{48,16},{56,24},{6... | collective-permute-start | bytes 786440 | tf_op jit(solution)/shard_map/ppermute | solution.py:346
  40.8 0.2 collective-permute-start.14
  41.0 0.9 collective-permute-done.12.rest_0_
  42.0 0.6 collective-permute-start.16
  42.6 0.2 collective-permute-done.15.rest_3_
  42.8 3.7 %collective-permute-start.17 = (bf16[2,512,128]{2,1,0:T(8,128)(2,1)S(1)}, bf16[2,512,128]{2,1,0:T(8,128)(2,1)S(1)}, u32[]{:S(2)}, u32[]{:S(2)}) collective-permute-start(bf16[2,512,128]{2,1,0:T(8,128)(2,1)S(1)} %collective-permute-done.15.rest_3_), channel_id=1, source_target_pairs={{0,224},{8,232},{16,240},{24,248},{32,0},{40,8},{48,16},{56,24},{6... | collective-permute-start | bytes 786440 | tf_op jit(solution)/shard_map/ppermute | solution.py:352
  46.5 13.8 %first.1 = (bf16[9,5,128,128]{3,2,1,0:T(8,128)(2,1)S(1)}, f32[9,5,128,128]{3,2,1,0:T(8,128)S(1)}, f32[9,8,128]{2,1,0:T(8,128)S(1)}, f32[9,8,128]{2,1,0:T(8,128)S(1)}) custom-call(s32[72]{0:T(128)S(1)} %pad_add_fusion.meta, bf16[2,5,128,128]{3,2,1,0:T(8,128)(2,1)S(1)} %get-tuple-element.32.q_own, f32[2,5,128,128]{3,2,1,0:T(8,128)S(1)} %get-tuple-element.33.acc_own, ...), custom_call_target="tpu_custom_call" | custom-call | flops 2013265920 | bytes 8388608 | tf_op jit(solution)/shard_map/first/pallas_call | solution.py:429
  60.3 5.3 %middle.2 = (f32[9,5,128,128]{3,2,1,0:T(8,128)S(1)}, f32[9,8,128]{2,1,0:T(8,128)S(1)}, f32[9,8,128]{2,1,0:T(8,128)S(1)}) custom-call(s32[72]{0:T(128)S(1)} %pad_add_fusion.meta, bf16[9,5,128,128]{3,2,1,0:T(8,128)(2,1)S(1)} %get-tuple-element.36.q_ref, f32[9,5,128,128]{3,2,1,0:T(8,128)S(1)} %get-tuple-element.37.acc_in, ...), custom_call_target="tpu_custom_call" | custom-call | flops 1342177280 | bytes 8388608 | tf_op jit(solution)/shard_map/middle/pallas_call | solution.py:442
  65.6 5.3 %middle.3 = (f32[9,5,128,128]{3,2,1,0:T(8,128)S(1)}, f32[9,8,128]{2,1,0:T(8,128)S(1)}, f32[9,8,128]{2,1,0:T(8,128)S(1)}) custom-call(s32[72]{0:T(128)S(1)} %pad_add_fusion.meta, bf16[9,5,128,128]{3,2,1,0:T(8,128)(2,1)S(1)} %get-tuple-element.36.q_ref, f32[9,5,128,128]{3,2,1,0:T(8,128)S(1)} %get-tuple-element.40.acc_in, ...), custom_call_target="tpu_custom_call" | custom-call | flops 1342177280 | bytes 8388608 | tf_op jit(solution)/shard_map/middle/pallas_call | solution.py:442
  70.9 3.0 %last.1 = (f32[2,5,128,128]{3,2,1,0:T(8,128)S(1)}, f32[2,8,128]{2,1,0:T(8,128)S(1)}, f32[2,8,128]{2,1,0:T(8,128)S(1)}, bf16[1376,128]{1,0:T(8,128)(2,1)S(1)}, bf...) custom-call(s32[72]{0:T(128)S(1)} %pad_add_fusion.meta, bf16[9,5,128,128]{3,2,1,0:T(8,128)(2,1)S(1)} %get-tuple-element.36.q_ref, ...), custom_call_target="tpu_custom_call" | custom-call | flops 671088640 | bytes 8388608 | tf_op jit(solution)/shard_map/last/pallas_call | solution.py:455
  73.9 0.8 copy-done
  74.7 0.6 copy-done.2
  75.3 0.6 copy-done.3
  75.9 1.9 %collective-permute-start.20 = (bf16[1376,128]{1,0:T(8,128)(2,1)S(1)}, bf16[1376,128]{1,0:T(8,128)(2,1)S(1)}, u32[]{:S(2)}, u32[]{:S(2)}) collective-permute-start(bf16[1376,128]{1,0:T(8,128)(2,1)S(1)} %get-tuple-element.51), channel_id=1, source_target_pairs={{0,24},{8,16},{16,8},{24,0},{32,56},{40,48},{48,40},{56,32},{64,88... | collective-permute-start | bytes 1056776 | tf_op jit(solution)/shard_map/ppermute | solution.py:476
  77.8 9.2 %collective-permute-done.19.o2 = bf16[1376,128]{1,0:T(8,128)(2,1)S(1)} collective-permute-done((bf16[1376,128]{1,0:T(8,128)(2,1)S(1)}, bf16[1376,128]{1,0:T(8,128)(2,1)S(1)}, u32[]{:S(2)}, u32[]{:S(2)}) %collective-permute-start.19) | collective-permute-done | bytes 352288 | tf_op jit(solution)/shard_map/ppermute | solution.py:476
  87.0 6.6 %collective-permute-done.20.o3 = bf16[1376,128]{1,0:T(8,128)(2,1)S(1)} collective-permute-done((bf16[1376,128]{1,0:T(8,128)(2,1)S(1)}, bf16[1376,128]{1,0:T(8,128)(2,1)S(1)}, u32[]{:S(2)}, u32[]{:S(2)}) %collective-permute-start.20) | collective-permute-done | bytes 352288 | tf_op jit(solution)/shard_map/ppermute | solution.py:476
  93.6 0.7 copy-done.10
  94.4 7.6 %combine.1 = (f32[256,640]{1,0:T(8,128)}, bf16[256,640]{1,0:T(8,128)(2,1)}, bf16[256,640]{1,0:T(8,128)(2,1)}, bf16[256,640]{1,0:T(8,128)(2,1)}, bf16[256,640]{1,...) custom-call(s32[72]{0:T(128)} %copy-done.1, s32[1]{0:T(128)} %bitcast.1.where, ...), custom_call_target="tpu_custom_call" | custom-call | flops 1677721600 | bytes 12582912 | tf_op jit(solution)/shard_map/combine/pallas_call | solution.py:481
  102.0 0.0 copy-start.11
  102.0 1.7 %collective-permute-start.21 = (bf16[256,640]{1,0:T(8,128)(2,1)}, bf16[256,640]{1,0:T(8,128)(2,1)S(1)}, u32[]{:S(2)}, u32[]{:S(2)}) collective-permute-start(bf16[256,640]{1,0:T(8,128)(2,1)} %get-tuple-element.53), channel_id=1, source_target_pairs={{0,1},{1,0},{2,3},{3,2},{4,5},{5,4},{6,7},{7,6},{8,9},{9,8},{10,11... | collective-permute-start | bytes 983048 | tf_op jit(solution)/shard_map/ppermute | solution.py:498
  103.7 2.9 %collective-permute-start.22 = (bf16[256,640]{1,0:T(8,128)(2,1)}, bf16[256,640]{1,0:T(8,128)(2,1)S(1)}, u32[]{:S(2)}, u32[]{:S(2)}) collective-permute-start(bf16[256,640]{1,0:T(8,128)(2,1)} %get-tuple-element.54), channel_id=1, source_target_pairs={{0,2},{1,3},{2,0},{3,1},{4,6},{5,7},{6,4},{7,5},{8,10},{9,11},{10,... | collective-permute-start | bytes 983048 | tf_op jit(solution)/shard_map/ppermute | solution.py:498
  106.6 0.2 collective-permute-start.23
  106.8 2.4 %collective-permute-start.24 = (bf16[256,640]{1,0:T(8,128)(2,1)}, bf16[256,640]{1,0:T(8,128)(2,1)S(1)}, u32[]{:S(2)}, u32[]{:S(2)}) collective-permute-start(bf16[256,640]{1,0:T(8,128)(2,1)} %get-tuple-element.56), channel_id=1, source_target_pairs={{0,4},{1,5},{2,6},{3,7},{4,0},{5,1},{6,2},{7,3},{8,12},{9,13},{10,... | collective-permute-start | bytes 983048 | tf_op jit(solution)/shard_map/ppermute | solution.py:498
  109.3 0.9 collective-permute-start.25
  110.2 2.8 %collective-permute-done.21 = bf16[256,640]{1,0:T(8,128)(2,1)S(1)} collective-permute-done((bf16[256,640]{1,0:T(8,128)(2,1)}, bf16[256,640]{1,0:T(8,128)(2,1)S(1)}, u32[]{:S(2)}, u32[]{:S(2)}) %collective-permute-start.21) | collective-permute-done | bytes 327712 | tf_op jit(solution)/shard_map/ppermute | solution.py:498
  112.9 5.0 %collective-permute-start.26 = (bf16[256,640]{1,0:T(8,128)(2,1)}, bf16[256,640]{1,0:T(8,128)(2,1)S(1)}, u32[]{:S(2)}, u32[]{:S(2)}) collective-permute-start(bf16[256,640]{1,0:T(8,128)(2,1)} %get-tuple-element.58), channel_id=1, source_target_pairs={{0,6},{1,7},{2,4},{3,5},{4,2},{5,3},{6,0},{7,1},{8,14},{9,15},{10,... | collective-permute-start | bytes 983048 | tf_op jit(solution)/shard_map/ppermute | solution.py:498
  118.0 17.8 %collective-permute-done.22 = bf16[256,640]{1,0:T(8,128)(2,1)S(1)} collective-permute-done((bf16[256,640]{1,0:T(8,128)(2,1)}, bf16[256,640]{1,0:T(8,128)(2,1)S(1)}, u32[]{:S(2)}, u32[]{:S(2)}) %collective-permute-start.22) | collective-permute-done | bytes 327712 | tf_op jit(solution)/shard_map/ppermute | solution.py:498
  135.8 2.1 %collective-permute-start.27 = (bf16[256,640]{1,0:T(8,128)(2,1)}, bf16[256,640]{1,0:T(8,128)(2,1)S(1)}, u32[]{:S(2)}, u32[]{:S(2)}) collective-permute-start(bf16[256,640]{1,0:T(8,128)(2,1)} %get-tuple-element.59), channel_id=1, source_target_pairs={{0,7},{1,6},{2,5},{3,4},{4,3},{5,2},{6,1},{7,0},{8,15},{9,14},{10,... | collective-permute-start | bytes 983048 | tf_op jit(solution)/shard_map/ppermute | solution.py:498
  137.9 10.8 %collective-permute-done.27 = bf16[256,640]{1,0:T(8,128)(2,1)S(1)} collective-permute-done((bf16[256,640]{1,0:T(8,128)(2,1)}, bf16[256,640]{1,0:T(8,128)(2,1)S(1)}, u32[]{:S(2)}, u32[]{:S(2)}) %collective-permute-start.27) | collective-permute-done | bytes 327712 | tf_op jit(solution)/shard_map/ppermute | solution.py:498
  148.7 1.6 fusion
  150.3 0.7 broadcast_in_dim.88
  151.0 3.7 %all-to-all-start = ((f32[8,8,128]{2,1,0:T(8,128)}), f32[8,8,128]{2,1,0:T(8,128)S(1)}, u32[]{:S(2)}, u32[]{:S(2)}) async-start(f32[8,8,128]{2,1,0:T(8,128)} %broadcast_in_dim.88), calls=%async_computation | async-start | bytes 65536 | tf_op jit(solution)/shard_map/all_to_all | solution.py:509
  154.7 7.7 %all-to-all-done = f32[8,8,128]{2,1,0:T(8,128)S(1)} async-done(((f32[8,8,128]{2,1,0:T(8,128)}), f32[8,8,128]{2,1,0:T(8,128)S(1)}, u32[]{:S(2)}, u32[]{:S(2)}) %all-to-all-start) | async-done | bytes 32800 | tf_op jit(solution)/shard_map/all_to_all | solution.py:509
  162.5 0.9 fusion.2
  (49 shorter events, 0.2 us)
Async XLA Ops:
  0.6 36.6 %copy-start.4 = (bf16[256,640]{1,0:T(8,128)(2,1)S(1)}, bf16[256,640]{1,0:T(8,128)(2,1)}, u32[]{:S(2)}) copy-start(bf16[256,640]{1,0:T(8,128)(2,1)} %q_in.1) | copy-start | bytes 983044
  0.6 36.6 %copy-start.5 = (bf16[256,128]{1,0:T(8,128)(2,1)S(1)}, bf16[256,128]{1,0:T(8,128)(2,1)}, u32[]{:S(2)}) copy-start(bf16[256,128]{1,0:T(8,128)(2,1)} %k_in.1) | copy-start | bytes 196612
  0.7 36.6 %copy-start.6 = (bf16[256,128]{1,0:T(8,128)(2,1)S(1)}, bf16[256,128]{1,0:T(8,128)(2,1)}, u32[]{:S(2)}) copy-start(bf16[256,128]{1,0:T(8,128)(2,1)} %v_in.1) | copy-start | bytes 196612
  2.8 12.8 %collective-permute-start.4 = (bf16[2,512,128]{2,1,0:T(8,128)(2,1)S(1)}, bf16[2,512,128]{2,1,0:T(8,128)(2,1)S(1)}, u32[]{:S(2)}, u32[]{:S(2)}) collective-permute-start(bf16[2,512,128]{2,1,0:T(8,128)(2,1)S(1)} %get-tuple-element.68.rest_0_), channel_id=1, source_target_pairs={{0,32},{8,40},{16,48},{24,56},{32,64},{40,72},{48,80},{56,88},{64,... | collective-permute-start | bytes 786440 | tf_op jit(solution)/shard_map/ppermute | solution.py:345
  4.7 10.9 %collective-permute-start.5 = (bf16[2,512,128]{2,1,0:T(8,128)(2,1)S(1)}, bf16[2,512,128]{2,1,0:T(8,128)(2,1)S(1)}, u32[]{:S(2)}, u32[]{:S(2)}) collective-permute-start(bf16[2,512,128]{2,1,0:T(8,128)(2,1)S(1)} %get-tuple-element.68.rest_0_), channel_id=1, source_target_pairs={{0,224},{8,232},{16,240},{24,248},{32,0},{40,8},{48,16},{56,24},{6... | collective-permute-start | bytes 786440 | tf_op jit(solution)/shard_map/ppermute | solution.py:346
  8.8 16.1 %collective-permute-start = (bf16[256,640]{1,0:T(8,128)(2,1)}, bf16[256,640]{1,0:T(8,128)(2,1)S(1)}, u32[]{:S(2)}, u32[]{:S(2)}) collective-permute-start(bf16[256,640]{1,0:T(8,128)(2,1)} %q_in.1), channel_id=1, source_target_pairs={{0,8},{8,0},{16,24},{24,16},{32,40},{40,32},{48,56},{56,48},{64,72... | collective-permute-start | bytes 983048 | tf_op jit(solution)/shard_map/ppermute | solution.py:337
  8.8 17.0 %collective-permute-start.1 = (bf16[256,640]{1,0:T(8,128)(2,1)}, bf16[256,640]{1,0:T(8,128)(2,1)S(1)}, u32[]{:S(2)}, u32[]{:S(2)}) collective-permute-start(bf16[256,640]{1,0:T(8,128)(2,1)} %q_in.1), channel_id=1, source_target_pairs={{0,16},{8,24},{16,0},{24,8},{32,48},{40,56},{48,32},{56,40},{64,80... | collective-permute-start | bytes 983048 | tf_op jit(solution)/shard_map/ppermute | solution.py:337
  9.3 3.9 %collective-permute-start.3 = (bf16[2,512,128]{2,1,0:T(8,128)(2,1)S(1)}, bf16[2,512,128]{2,1,0:T(8,128)(2,1)S(1)}, u32[]{:S(2)}, u32[]{:S(2)}) collective-permute-start(bf16[2,512,128]{2,1,0:T(8,128)(2,1)S(1)} %get-tuple-element.67), channel_id=1, source_target_pairs={{0,8},{8,0},{16,24},{24,16},{32,40},{40,32},{48,56},{56,48},{64,72... | collective-permute-start | bytes 786440 | tf_op jit(solution)/shard_map/ppermute | solution.py:336
  13.2 8.5 %collective-permute-start.7 = (bf16[2,512,128]{2,1,0:T(8,128)(2,1)S(1)}, bf16[2,512,128]{2,1,0:T(8,128)(2,1)S(1)}, u32[]{:S(2)}, u32[]{:S(2)}) collective-permute-start(bf16[2,512,128]{2,1,0:T(8,128)(2,1)S(1)} %collective-permute-done.3.rest_1_), channel_id=1, source_target_pairs={{0,224},{8,232},{16,240},{24,248},{32,0},{40,8},{48,16},{56,24},{6... | collective-permute-start | bytes 786440 | tf_op jit(solution)/shard_map/ppermute | solution.py:346
  15.5 10.7 %collective-permute-start.6 = (bf16[2,512,128]{2,1,0:T(8,128)(2,1)S(1)}, bf16[2,512,128]{2,1,0:T(8,128)(2,1)S(1)}, u32[]{:S(2)}, u32[]{:S(2)}) collective-permute-start(bf16[2,512,128]{2,1,0:T(8,128)(2,1)S(1)} %collective-permute-done.3.rest_1_), channel_id=1, source_target_pairs={{0,32},{8,40},{16,48},{24,56},{32,64},{40,72},{48,80},{56,88},{64,... | collective-permute-start | bytes 786440 | tf_op jit(solution)/shard_map/ppermute | solution.py:345
  15.7 14.9 %collective-permute-start.8 = (bf16[2,512,128]{2,1,0:T(8,128)(2,1)S(1)}, bf16[2,512,128]{2,1,0:T(8,128)(2,1)S(1)}, u32[]{:S(2)}, u32[]{:S(2)}) collective-permute-start(bf16[2,512,128]{2,1,0:T(8,128)(2,1)S(1)} %collective-permute-done.4.rest_2_), channel_id=1, source_target_pairs={{0,32},{8,40},{16,48},{24,56},{32,64},{40,72},{48,80},{56,88},{64,... | collective-permute-start | bytes 786440 | tf_op jit(solution)/shard_map/ppermute | solution.py:345
  21.7 9.8 %collective-permute-start.11 = (bf16[2,512,128]{2,1,0:T(8,128)(2,1)S(1)}, bf16[2,512,128]{2,1,0:T(8,128)(2,1)S(1)}, u32[]{:S(2)}, u32[]{:S(2)}) collective-permute-start(bf16[2,512,128]{2,1,0:T(8,128)(2,1)S(1)} %collective-permute-done.7.rest_5_), channel_id=1, source_target_pairs={{0,224},{8,232},{16,240},{24,248},{32,0},{40,8},{48,16},{56,24},{6... | collective-permute-start | bytes 786440 | tf_op jit(solution)/shard_map/ppermute | solution.py:346
  24.9 21.6 %collective-permute-start.2 = (bf16[256,640]{1,0:T(8,128)(2,1)}, bf16[256,640]{1,0:T(8,128)(2,1)S(1)}, u32[]{:S(2)}, u32[]{:S(2)}) collective-permute-start(bf16[256,640]{1,0:T(8,128)(2,1)} %q_in.1), channel_id=1, source_target_pairs={{0,24},{8,16},{16,8},{24,0},{32,56},{40,48},{48,40},{56,32},{64,88... | collective-permute-start | bytes 983048 | tf_op jit(solution)/shard_map/ppermute | solution.py:337
  25.8 12.9 %collective-permute-start.9 = (bf16[2,512,128]{2,1,0:T(8,128)(2,1)S(1)}, bf16[2,512,128]{2,1,0:T(8,128)(2,1)S(1)}, u32[]{:S(2)}, u32[]{:S(2)}) collective-permute-start(bf16[2,512,128]{2,1,0:T(8,128)(2,1)S(1)} %collective-permute-done.5.rest_3_), channel_id=1, source_target_pairs={{0,224},{8,232},{16,240},{24,248},{32,0},{40,8},{48,16},{56,24},{6... | collective-permute-start | bytes 786440 | tf_op jit(solution)/shard_map/ppermute | solution.py:346
  26.2 14.7 %collective-permute-start.10 = (bf16[2,512,128]{2,1,0:T(8,128)(2,1)S(1)}, bf16[2,512,128]{2,1,0:T(8,128)(2,1)S(1)}, u32[]{:S(2)}, u32[]{:S(2)}) collective-permute-start(bf16[2,512,128]{2,1,0:T(8,128)(2,1)S(1)} %collective-permute-done.6.rest_4_), channel_id=1, source_target_pairs={{0,32},{8,40},{16,48},{24,56},{32,64},{40,72},{48,80},{56,88},{64,... | collective-permute-start | bytes 786440 | tf_op jit(solution)/shard_map/ppermute | solution.py:345
  30.6 11.3 %collective-permute-start.12 = (bf16[2,512,128]{2,1,0:T(8,128)(2,1)S(1)}, bf16[2,512,128]{2,1,0:T(8,128)(2,1)S(1)}, u32[]{:S(2)}, u32[]{:S(2)}) collective-permute-start(bf16[2,512,128]{2,1,0:T(8,128)(2,1)S(1)} %collective-permute-done.8.rest_0_), channel_id=1, source_target_pairs={{0,32},{8,40},{16,48},{24,56},{32,64},{40,72},{48,80},{56,88},{64,... | collective-permute-start | bytes 786440 | tf_op jit(solution)/shard_map/ppermute | solution.py:345
  31.5 11.2 %collective-permute-start.15 = (bf16[2,512,128]{2,1,0:T(8,128)(2,1)S(1)}, bf16[2,512,128]{2,1,0:T(8,128)(2,1)S(1)}, u32[]{:S(2)}, u32[]{:S(2)}) collective-permute-start(bf16[2,512,128]{2,1,0:T(8,128)(2,1)S(1)} %collective-permute-done.11.rest_3_), channel_id=1, source_target_pairs={{0,224},{8,232},{16,240},{24,248},{32,0},{40,8},{48,16},{56,24},{6... | collective-permute-start | bytes 786440 | tf_op jit(solution)/shard_map/ppermute | solution.py:346
  36.0 34.9 %copy-start.1 = (s32[72]{0:T(128)}, s32[72]{0:T(128)S(1)}, u32[]{:S(2)}) copy-start(s32[72]{0:T(128)S(1)} %pad_add_fusion.meta) | copy-start | bytes 868
  38.7 26.8 %collective-permute-start.13 = (bf16[2,512,128]{2,1,0:T(8,128)(2,1)S(1)}, bf16[2,512,128]{2,1,0:T(8,128)(2,1)S(1)}, u32[]{:S(2)}, u32[]{:S(2)}) collective-permute-start(bf16[2,512,128]{2,1,0:T(8,128)(2,1)S(1)} %collective-permute-done.9.rest_1_), channel_id=1, source_target_pairs={{0,224},{8,232},{16,240},{24,248},{32,0},{40,8},{48,16},{56,24},{6... | collective-permute-start | bytes 786440 | tf_op jit(solution)/shard_map/ppermute | solution.py:346
  40.8 24.7 %collective-permute-start.14 = (bf16[2,512,128]{2,1,0:T(8,128)(2,1)S(1)}, bf16[2,512,128]{2,1,0:T(8,128)(2,1)S(1)}, u32[]{:S(2)}, u32[]{:S(2)}) collective-permute-start(bf16[2,512,128]{2,1,0:T(8,128)(2,1)S(1)} %collective-permute-done.10.rest_2_), channel_id=1, source_target_pairs={{0,32},{8,40},{16,48},{24,56},{32,64},{40,72},{48,80},{56,88},{64,... | collective-permute-start | bytes 786440 | tf_op jit(solution)/shard_map/ppermute | solution.py:345
  42.0 28.9 %collective-permute-start.16 = (bf16[2,512,128]{2,1,0:T(8,128)(2,1)S(1)}, bf16[2,512,128]{2,1,0:T(8,128)(2,1)S(1)}, u32[]{:S(2)}, u32[]{:S(2)}) collective-permute-start(bf16[2,512,128]{2,1,0:T(8,128)(2,1)S(1)} %collective-permute-done.12.rest_0_), channel_id=1, source_target_pairs={{0,32},{8,40},{16,48},{24,56},{32,64},{40,72},{48,80},{56,88},{64,... | collective-permute-start | bytes 786440 | tf_op jit(solution)/shard_map/ppermute | solution.py:350
  42.8 28.1 %collective-permute-start.17 = (bf16[2,512,128]{2,1,0:T(8,128)(2,1)S(1)}, bf16[2,512,128]{2,1,0:T(8,128)(2,1)S(1)}, u32[]{:S(2)}, u32[]{:S(2)}) collective-permute-start(bf16[2,512,128]{2,1,0:T(8,128)(2,1)S(1)} %collective-permute-done.15.rest_3_), channel_id=1, source_target_pairs={{0,224},{8,232},{16,240},{24,248},{32,0},{40,8},{48,16},{56,24},{6... | collective-permute-start | bytes 786440 | tf_op jit(solution)/shard_map/ppermute | solution.py:352
  73.9 0.8 copy-start
  74.7 0.6 copy-start.2
  75.3 0.6 copy-start.3
  75.9 1.9 %collective-permute-start.18 = (bf16[1376,128]{1,0:T(8,128)(2,1)S(1)}, bf16[1376,128]{1,0:T(8,128)(2,1)S(1)}, u32[]{:S(2)}, u32[]{:S(2)}) collective-permute-start(bf16[1376,128]{1,0:T(8,128)(2,1)S(1)} %get-tuple-element.49), channel_id=1, source_target_pairs={{0,8},{8,0},{16,24},{24,16},{32,40},{40,32},{48,56},{56,48},{64,72... | collective-permute-start | bytes 1056776 | tf_op jit(solution)/shard_map/ppermute | solution.py:476
  75.9 11.1 %collective-permute-start.19 = (bf16[1376,128]{1,0:T(8,128)(2,1)S(1)}, bf16[1376,128]{1,0:T(8,128)(2,1)S(1)}, u32[]{:S(2)}, u32[]{:S(2)}) collective-permute-start(bf16[1376,128]{1,0:T(8,128)(2,1)S(1)} %get-tuple-element.50), channel_id=1, source_target_pairs={{0,16},{8,24},{16,0},{24,8},{32,48},{40,56},{48,32},{56,40},{64,80... | collective-permute-start | bytes 1056776 | tf_op jit(solution)/shard_map/ppermute | solution.py:476
  75.9 17.7 %collective-permute-start.20 = (bf16[1376,128]{1,0:T(8,128)(2,1)S(1)}, bf16[1376,128]{1,0:T(8,128)(2,1)S(1)}, u32[]{:S(2)}, u32[]{:S(2)}) collective-permute-start(bf16[1376,128]{1,0:T(8,128)(2,1)S(1)} %get-tuple-element.51), channel_id=1, source_target_pairs={{0,24},{8,16},{16,8},{24,0},{32,56},{40,48},{48,40},{56,32},{64,88... | collective-permute-start | bytes 1056776 | tf_op jit(solution)/shard_map/ppermute | solution.py:476
  77.8 15.9 %copy-start.8 = (bf16[1376,128]{1,0:T(8,128)(2,1)}, bf16[1376,128]{1,0:T(8,128)(2,1)S(1)}, u32[]{:S(2)}) copy-start(bf16[1376,128]{1,0:T(8,128)(2,1)S(1)} %collective-permute-done.18.o1) | copy-start | bytes 1056772
  87.0 6.6 %copy-start.9 = (bf16[1376,128]{1,0:T(8,128)(2,1)}, bf16[1376,128]{1,0:T(8,128)(2,1)S(1)}, u32[]{:S(2)}) copy-start(bf16[1376,128]{1,0:T(8,128)(2,1)S(1)} %collective-permute-done.19.o2) | copy-start | bytes 1056772
  93.6 0.7 copy-start.10
  102.0 52.7 %copy-start.11 = (bf16[640]{0:T(1024)(128)(2,1)S(1)}, bf16[640]{0:T(1024)(128)(2,1)}, u32[]{:S(2)}) copy-start(bf16[640]{0:T(1024)(128)(2,1)} %param.21) | copy-start | bytes 3844
  102.0 10.9 %collective-permute-start.21 = (bf16[256,640]{1,0:T(8,128)(2,1)}, bf16[256,640]{1,0:T(8,128)(2,1)S(1)}, u32[]{:S(2)}, u32[]{:S(2)}) collective-permute-start(bf16[256,640]{1,0:T(8,128)(2,1)} %get-tuple-element.53), channel_id=1, source_target_pairs={{0,1},{1,0},{2,3},{3,2},{4,5},{5,4},{6,7},{7,6},{8,9},{9,8},{10,11... | collective-permute-start | bytes 983048 | tf_op jit(solution)/shard_map/ppermute | solution.py:498
  103.7 32.1 %collective-permute-start.22 = (bf16[256,640]{1,0:T(8,128)(2,1)}, bf16[256,640]{1,0:T(8,128)(2,1)S(1)}, u32[]{:S(2)}, u32[]{:S(2)}) collective-permute-start(bf16[256,640]{1,0:T(8,128)(2,1)} %get-tuple-element.54), channel_id=1, source_target_pairs={{0,2},{1,3},{2,0},{3,1},{4,6},{5,7},{6,4},{7,5},{8,10},{9,11},{10,... | collective-permute-start | bytes 983048 | tf_op jit(solution)/shard_map/ppermute | solution.py:498
  106.6 31.3 %collective-permute-start.23 = (bf16[256,640]{1,0:T(8,128)(2,1)}, bf16[256,640]{1,0:T(8,128)(2,1)S(1)}, u32[]{:S(2)}, u32[]{:S(2)}) collective-permute-start(bf16[256,640]{1,0:T(8,128)(2,1)} %get-tuple-element.55), channel_id=1, source_target_pairs={{0,3},{1,2},{2,1},{3,0},{4,7},{5,6},{6,5},{7,4},{8,11},{9,10},{10,... | collective-permute-start | bytes 983048 | tf_op jit(solution)/shard_map/ppermute | solution.py:498
  106.8 31.1 %collective-permute-start.24 = (bf16[256,640]{1,0:T(8,128)(2,1)}, bf16[256,640]{1,0:T(8,128)(2,1)S(1)}, u32[]{:S(2)}, u32[]{:S(2)}) collective-permute-start(bf16[256,640]{1,0:T(8,128)(2,1)} %get-tuple-element.56), channel_id=1, source_target_pairs={{0,4},{1,5},{2,6},{3,7},{4,0},{5,1},{6,2},{7,3},{8,12},{9,13},{10,... | collective-permute-start | bytes 983048 | tf_op jit(solution)/shard_map/ppermute | solution.py:498
  109.3 28.6 %collective-permute-start.25 = (bf16[256,640]{1,0:T(8,128)(2,1)}, bf16[256,640]{1,0:T(8,128)(2,1)S(1)}, u32[]{:S(2)}, u32[]{:S(2)}) collective-permute-start(bf16[256,640]{1,0:T(8,128)(2,1)} %get-tuple-element.57), channel_id=1, source_target_pairs={{0,5},{1,4},{2,7},{3,6},{4,1},{5,0},{6,3},{7,2},{8,13},{9,12},{10,... | collective-permute-start | bytes 983048 | tf_op jit(solution)/shard_map/ppermute | solution.py:498
  112.9 25.0 %collective-permute-start.26 = (bf16[256,640]{1,0:T(8,128)(2,1)}, bf16[256,640]{1,0:T(8,128)(2,1)S(1)}, u32[]{:S(2)}, u32[]{:S(2)}) collective-permute-start(bf16[256,640]{1,0:T(8,128)(2,1)} %get-tuple-element.58), channel_id=1, source_target_pairs={{0,6},{1,7},{2,4},{3,5},{4,2},{5,3},{6,0},{7,1},{8,14},{9,15},{10,... | collective-permute-start | bytes 983048 | tf_op jit(solution)/shard_map/ppermute | solution.py:498
  135.8 12.9 %collective-permute-start.27 = (bf16[256,640]{1,0:T(8,128)(2,1)}, bf16[256,640]{1,0:T(8,128)(2,1)S(1)}, u32[]{:S(2)}, u32[]{:S(2)}) collective-permute-start(bf16[256,640]{1,0:T(8,128)(2,1)} %get-tuple-element.59), channel_id=1, source_target_pairs={{0,7},{1,6},{2,5},{3,4},{4,3},{5,2},{6,1},{7,0},{8,15},{9,14},{10,... | collective-permute-start | bytes 983048 | tf_op jit(solution)/shard_map/ppermute | solution.py:498
  150.3 13.0 %copy-start.7 = (bf16[256,640]{1,0:T(8,128)(2,1)}, bf16[256,640]{1,0:T(8,128)(2,1)S(1)}, u32[]{:S(2)}) copy-start(bf16[256,640]{1,0:T(8,128)(2,1)S(1)} %get-tuple-element.66) | copy-start | bytes 983044
  151.0 11.5 %all-to-all-start = ((f32[8,8,128]{2,1,0:T(8,128)}), f32[8,8,128]{2,1,0:T(8,128)S(1)}, u32[]{:S(2)}, u32[]{:S(2)}) async-start(f32[8,8,128]{2,1,0:T(8,128)} %broadcast_in_dim.88), calls=%async_computation | async-start | bytes 65536 | tf_op jit(solution)/shard_map/all_to_all | solution.py:509
where the time goes:
time: 164 us; the launch traced here: 163 us
  waiting for transfers between devices  65.7 us (40%)
  starting transfers between devices  45.6 us (28%)
  Pallas kernels  36.5 us (22%)
  other arithmetic  9.08 us (6%)
  local copies, waits for them, and re-layouts  5.59 us (3%)
    ppermute x7, waiting for transfers between devices, shards(): lax.ppermute(pieces[k], 'tp', [(i, i ^ k) for i in range(ways)])  31.4 us
    ppermute x3, waiting for transfers between devices, shards(): lax.ppermute(out, 'req', beside(k))  15.9 us
    ppermute x6, starting transfers between devices, shards(): moving_down = lax.ppermute(moving_down, 'req', down_pairs)  15.3 us
    ppermute x7, starting transfers between devices, shards(): lax.ppermute(pieces[k], 'tp', [(i, i ^ k) for i in range(ways)])  15.2 us
    pallas_call x1, Pallas kernels, shards(): pl.pallas_call(make_first(base, len(parts)), out_shape=(shape((every, hea...  13.8 us
    pallas_call x2, Pallas kernels, shards(): pl.pallas_call(make_middle(base, len(parts)), out_shape=state_shapes, in_...  10.5 us
    all_to_all x1, waiting for transfers between devices, shards(): lax.all_to_all(jnp.broadcast_to(squares[None], (ways, 8, HD)), 'tp', 0, 0)  7.75 us
    pallas_call x1, Pallas kernels, shards(): pl.pallas_call(combine_kernel, out_shape=tuple((shape((slots, columns), b...  7.64 us
  transfers between devices with their start and end apart: 29, of which 11 were waited for; matrix products, arithmetic and copies ran while one was open for 4% of the time, Pallas kernels for 16%

commit v1 on v0

--- a/solution.py
+++ b/solution.py
@@ -24,7 +24,7 @@
     return pl.BlockSpec(memory_space=space)
 
 
-def params(limit=40):
+def params(limit=26):
     return pltpu.CompilerParams(vmem_limit_bytes=limit * 1024 * 1024)
 
 
@@ -235,11 +235,20 @@
     return kernel
 
 
-def combine_kernel(meta, where, acc_own, max_own, sum_own, o1, o2, o3, weight_in, *rest):
-    ways = (len(rest) - 3)
+def combine_kernel(meta, where, acc_in, max_in, sum_in, r1, r2, r3, weight_in, *rest):
+    received = (r1, r2, r3)
+    ways = len(rest) - 10
     outs = rest[:ways]
-    attn_ref, weight_ref, sems = rest[ways:]
+    attn_ref, weight_ref, sems, part_sems, acc_own, max_own, sum_own, o1, o2, o3 = rest[ways:]
     columns = weight_ref.shape[2]
+    parts = (acc_in, max_in, sum_in, *received)
+    held = (acc_own, max_own, sum_own, o1, o2, o3)
+    early = [
+        pltpu.make_async_copy(source, target, part_sems.at[n])
+        for n, (source, target) in enumerate(zip(parts, held))
+    ]
+    for copy in early:
+        copy.start()
     copies = []
     for k in range(ways):
         at = pl.multiple_of((where[0] ^ k) * columns, HD)
@@ -250,6 +259,8 @@
         )
     for copy in copies[1:] + copies[:1]:
         copy.start()
+    for copy in early:
+        copy.wait()
     tiles, heads = acc_own.shape[:2]
     rows = 8 * tiles
     maxima = [jnp.concatenate([max_own[j] for j in range(tiles)], axis=0)]
@@ -334,7 +345,9 @@
     mine = lax.dynamic_slice_in_dim(both, core * part, part, 1)
     theirs = lax.dynamic_slice_in_dim(both, (1 - core) * part, part, 1)
     lanes = [mine, lax.ppermute(theirs, "req", beside(1))]
-    queries = [lax.ppermute(suffix_query, "req", beside(k)) for k in range(1, PLANE)]
+    queries = []
+    for k in range(1, PLANE):
+        queries.append(lax.ppermute(suffix_query, "req", beside(k)))
 
     entries = {(0, 0): lanes[0], (0, 1): lanes[1]}
     half_way = planes // 2
@@ -481,23 +494,27 @@
     pieces = pl.pallas_call(
         combine_kernel,
         out_shape=tuple(shape((slots, columns), bf16 if k else f32) for k in range(ways)),
-        in_specs=[full(SMEM)] * 2 + [full()] * 6 + [full(pl.ANY)],
+        in_specs=[full(SMEM)] * 2 + [full(pl.ANY)] * 6 + [full(pltpu.HBM)],
         out_specs=(full(),) * ways,
         scratch_shapes=[
             pltpu.VMEM((slots, heads * HD), bf16),
             pltpu.VMEM((ways, heads * HD, columns), bf16),
             pltpu.SemaphoreType.DMA((ways,)),
-        ],
+            pltpu.SemaphoreType.DMA((6,)),
+            pltpu.VMEM((tiles_each, heads, HD, TILE), f32),
+            pltpu.VMEM((tiles_each, 8, TILE), f32),
+            pltpu.VMEM((tiles_each, 8, TILE), f32),
+        ]
+        + [pltpu.VMEM((packed, HD), bf16)] * 3,
         cost_estimate=pl.CostEstimate(
             flops=2 * slots * heads * HD * width, bytes_accessed=12 << 20, transcendentals=0
         ),
-        compiler_params=params(60),
+        compiler_params=params(26),
         name="combine",
     )(meta, where, *last[:3], *returned, out_weight)
-    sent = [
-        lax.ppermute(pieces[k], "tp", [(i, i ^ k) for i in range(ways)])
-        for k in range(1, ways)
-    ]
+    sent = []
+    for k in range(1, ways):
+        sent.append(lax.ppermute(pieces[k], "tp", [(i, i ^ k) for i in range(ways)]))
     shared = pieces[0]
     for piece in sent:
         shared = shared + piece.astype(f32)

time: 164 us -> 163 us (level)
    unnamed x25 -> x13, local copies, waits for them, and re-layouts: 3.8 us -> 3.9 us
  transfers between devices with their start and end apart: 29 -> 29, of which waited for: 11 -> 10; matrix products, arithmetic and copies ran while one was open for 4% -> 4% of each run, Pallas kernels for 16% -> 16%
where the time goes in v1:
time: 163 us; the launch traced here: 162 us
  waiting for transfers between devices  65.5 us (40%)
  starting transfers between devices  45.3 us (28%)
  Pallas kernels  35.3 us (22%)
  other arithmetic  9.07 us (6%)
  local copies, waits for them, and re-layouts  6.2 us (4%)
    ppermute x7, waiting for transfers between devices, shards(): lax.ppermute(pieces[k], 'tp', [(i, i ^ k) for i in range(ways)])  31.7 us
    ppermute x3, waiting for transfers between devices, shards(): lax.ppermute(out, 'req', beside(k))  15.6 us
    ppermute x7, starting transfers between devices, shards(): lax.ppermute(pieces[k], 'tp', [(i, i ^ k) for i in range(ways)])  15.2 us
    ppermute x6, starting transfers between devices, shards(): moving_down = lax.ppermute(moving_down, 'req', down_pairs)  15.2 us
    pallas_call x1, Pallas kernels, shards(): pl.pallas_call(make_first(base, len(parts)), out_shape=(shape((every, hea...  13.7 us
    pallas_call x2, Pallas kernels, shards(): pl.pallas_call(make_middle(base, len(parts)), out_shape=state_shapes, in_...  10.4 us
    all_to_all x1, waiting for transfers between devices, shards(): lax.all_to_all(jnp.broadcast_to(squares[None], (ways, 8, HD)), 'tp', 0, 0)  7.75 us
    ppermute x6, waiting for transfers between devices, shards(): moving_down = lax.ppermute(moving_down, 'req', down_pairs)  6.83 us
  transfers between devices with their start and end apart: 29, of which 10 were waited for; matrix products, arithmetic and copies ran while one was open for 4% of the time, Pallas kernels for 16%

profile of v1, /device:TPU:2, one launch (start us, length us, event | category | flops | bytes accessed | tf_op | source)
XLA Modules:
  0.0 162.3 jit_solution(4095147614413456594)
XLA Ops:
  0.6 0.0 copy-start.1
  0.7 1.0 constant_dynamic-update-slice_fusion.1
  1.7 1.0 constant_dynamic-update-slice_fusion
  2.8 2.0 %collective-permute-start.4 = (bf16[2,512,128]{2,1,0:T(8,128)(2,1)S(1)}, bf16[2,512,128]{2,1,0:T(8,128)(2,1)S(1)}, u32[]{:S(2)}, u32[]{:S(2)}) collective-permute-start(bf16[2,512,128]{2,1,0:T(8,128)(2,1)S(1)} %get-tuple-element.68.rest_0_), channel_id=1, source_target_pairs={{0,32},{8,40},{16,48},{24,56},{32,64},{40,72},{48,80},{56,88},{64,... | collective-permute-start | bytes 786440 | tf_op jit(solution)/shard_map/ppermute | solution.py:358
  4.7 4.0 %collective-permute-start.5 = (bf16[2,512,128]{2,1,0:T(8,128)(2,1)S(1)}, bf16[2,512,128]{2,1,0:T(8,128)(2,1)S(1)}, u32[]{:S(2)}, u32[]{:S(2)}) collective-permute-start(bf16[2,512,128]{2,1,0:T(8,128)(2,1)S(1)} %get-tuple-element.68.rest_0_), channel_id=1, source_target_pairs={{0,224},{8,232},{16,240},{24,248},{32,0},{40,8},{48,16},{56,24},{6... | collective-permute-start | bytes 786440 | tf_op jit(solution)/shard_map/ppermute | solution.py:359
  8.8 0.0 collective-permute-start
  8.8 0.5 collective-permute-start.1
  9.3 0.2 collective-permute-start.3
  9.5 0.8 select_reduce_fusion.1
  10.3 0.9 select_reduce_fusion.2
  11.2 0.7 fusion.6
  11.9 1.3 fusion.3
  13.2 0.0 collective-permute-done.3.rest_1_
  13.2 1.9 %collective-permute-start.7 = (bf16[2,512,128]{2,1,0:T(8,128)(2,1)S(1)}, bf16[2,512,128]{2,1,0:T(8,128)(2,1)S(1)}, u32[]{:S(2)}, u32[]{:S(2)}) collective-permute-start(bf16[2,512,128]{2,1,0:T(8,128)(2,1)S(1)} %collective-permute-done.3.rest_1_), channel_id=1, source_target_pairs={{0,224},{8,232},{16,240},{24,248},{32,0},{40,8},{48,16},{56,24},{6... | collective-permute-start | bytes 786440 | tf_op jit(solution)/shard_map/ppermute | solution.py:359
  15.1 0.2 select_reduce_fusion.5
  15.3 0.2 select_reduce_fusion.3
  15.5 0.2 collective-permute-start.6
  15.7 0.1 collective-permute-start.8
  15.8 5.9 %collective-permute-done.7.rest_5_ = bf16[2,512,128]{2,1,0:T(8,128)(2,1)S(1)} collective-permute-done((bf16[2,512,128]{2,1,0:T(8,128)(2,1)S(1)}, bf16[2,512,128]{2,1,0:T(8,128)(2,1)S(1)}, u32[]{:S(2)}, u32[]{:S(2)}) %collective-permute-start.7) | collective-permute-done | bytes 262176 | tf_op jit(solution)/shard_map/ppermute | solution.py:359
  21.7 3.1 %collective-permute-start.11 = (bf16[2,512,128]{2,1,0:T(8,128)(2,1)S(1)}, bf16[2,512,128]{2,1,0:T(8,128)(2,1)S(1)}, u32[]{:S(2)}, u32[]{:S(2)}) collective-permute-start(bf16[2,512,128]{2,1,0:T(8,128)(2,1)S(1)} %collective-permute-done.7.rest_5_), channel_id=1, source_target_pairs={{0,224},{8,232},{16,240},{24,248},{32,0},{40,8},{48,16},{56,24},{6... | collective-permute-start | bytes 786440 | tf_op jit(solution)/shard_map/ppermute | solution.py:359
  24.8 0.1 compare_convert_fusion
  24.9 0.3 collective-permute-start.2
  25.2 0.5 and_select_fusion.2
  25.7 0.6 reshape.77
  26.3 0.3 collective-permute-start.9
  26.6 1.7 %collective-permute-start.10 = (bf16[2,512,128]{2,1,0:T(8,128)(2,1)S(1)}, bf16[2,512,128]{2,1,0:T(8,128)(2,1)S(1)}, u32[]{:S(2)}, u32[]{:S(2)}) collective-permute-start(bf16[2,512,128]{2,1,0:T(8,128)(2,1)S(1)} %collective-permute-done.6.rest_4_), channel_id=1, source_target_pairs={{0,32},{8,40},{16,48},{24,56},{32,64},{40,72},{48,80},{56,88},{64,... | collective-permute-start | bytes 786440 | tf_op jit(solution)/shard_map/ppermute | solution.py:358
  28.3 2.3 %collective-permute-done.8.rest_0_ = bf16[2,512,128]{2,1,0:T(8,128)(2,1)S(1)} collective-permute-done((bf16[2,512,128]{2,1,0:T(8,128)(2,1)S(1)}, bf16[2,512,128]{2,1,0:T(8,128)(2,1)S(1)}, u32[]{:S(2)}, u32[]{:S(2)}) %collective-permute-start.8) | collective-permute-done | bytes 262176 | tf_op jit(solution)/shard_map/ppermute | solution.py:358
  30.6 0.9 collective-permute-done.11.rest_3_
  31.5 3.7 %collective-permute-start.15 = (bf16[2,512,128]{2,1,0:T(8,128)(2,1)S(1)}, bf16[2,512,128]{2,1,0:T(8,128)(2,1)S(1)}, u32[]{:S(2)}, u32[]{:S(2)}) collective-permute-start(bf16[2,512,128]{2,1,0:T(8,128)(2,1)S(1)} %collective-permute-done.11.rest_3_), channel_id=1, source_target_pairs={{0,224},{8,232},{16,240},{24,248},{32,0},{40,8},{48,16},{56,24},{6... | collective-permute-start | bytes 786440 | tf_op jit(solution)/shard_map/ppermute | solution.py:359
  35.2 0.7 pad_add_fusion.meta
  36.0 1.2 pad_maximum_fusion
  37.2 1.5 own.1
  38.7 2.1 %collective-permute-start.13 = (bf16[2,512,128]{2,1,0:T(8,128)(2,1)S(1)}, bf16[2,512,128]{2,1,0:T(8,128)(2,1)S(1)}, u32[]{:S(2)}, u32[]{:S(2)}) collective-permute-start(bf16[2,512,128]{2,1,0:T(8,128)(2,1)S(1)} %collective-permute-done.9.rest_1_), channel_id=1, source_target_pairs={{0,224},{8,232},{16,240},{24,248},{32,0},{40,8},{48,16},{56,24},{6... | collective-permute-start | bytes 786440 | tf_op jit(solution)/shard_map/ppermute | solution.py:359
  40.8 0.2 collective-permute-start.14
  41.0 1.4 collective-permute-done.12.rest_0_
  42.4 0.6 collective-permute-start.16
  43.0 3.5 %collective-permute-start.17 = (bf16[2,512,128]{2,1,0:T(8,128)(2,1)S(1)}, bf16[2,512,128]{2,1,0:T(8,128)(2,1)S(1)}, u32[]{:S(2)}, u32[]{:S(2)}) collective-permute-start(bf16[2,512,128]{2,1,0:T(8,128)(2,1)S(1)} %collective-permute-done.15.rest_3_), channel_id=1, source_target_pairs={{0,224},{8,232},{16,240},{24,248},{32,0},{40,8},{48,16},{56,24},{6... | collective-permute-start | bytes 786440 | tf_op jit(solution)/shard_map/ppermute | solution.py:365
  46.5 13.7 %first.1 = (bf16[9,5,128,128]{3,2,1,0:T(8,128)(2,1)S(1)}, f32[9,5,128,128]{3,2,1,0:T(8,128)S(1)}, f32[9,8,128]{2,1,0:T(8,128)S(1)}, f32[9,8,128]{2,1,0:T(8,128)S(1)}) custom-call(s32[72]{0:T(128)S(1)} %pad_add_fusion.meta, bf16[2,5,128,128]{3,2,1,0:T(8,128)(2,1)S(1)} %get-tuple-element.32.q_own, f32[2,5,128,128]{3,2,1,0:T(8,128)S(1)} %get-tuple-element.33.acc_own, ...), custom_call_target="tpu_custom_call" | custom-call | flops 2013265920 | bytes 8388608 | tf_op jit(solution)/shard_map/first/pallas_call | solution.py:442
  60.1 5.2 %middle.2 = (f32[9,5,128,128]{3,2,1,0:T(8,128)S(1)}, f32[9,8,128]{2,1,0:T(8,128)S(1)}, f32[9,8,128]{2,1,0:T(8,128)S(1)}) custom-call(s32[72]{0:T(128)S(1)} %pad_add_fusion.meta, bf16[9,5,128,128]{3,2,1,0:T(8,128)(2,1)S(1)} %get-tuple-element.36.q_ref, f32[9,5,128,128]{3,2,1,0:T(8,128)S(1)} %get-tuple-element.37.acc_in, ...), custom_call_target="tpu_custom_call" | custom-call | flops 1342177280 | bytes 8388608 | tf_op jit(solution)/shard_map/middle/pallas_call | solution.py:455
  65.4 5.2 %middle.3 = (f32[9,5,128,128]{3,2,1,0:T(8,128)S(1)}, f32[9,8,128]{2,1,0:T(8,128)S(1)}, f32[9,8,128]{2,1,0:T(8,128)S(1)}) custom-call(s32[72]{0:T(128)S(1)} %pad_add_fusion.meta, bf16[9,5,128,128]{3,2,1,0:T(8,128)(2,1)S(1)} %get-tuple-element.36.q_ref, f32[9,5,128,128]{3,2,1,0:T(8,128)S(1)} %get-tuple-element.40.acc_in, ...), custom_call_target="tpu_custom_call" | custom-call | flops 1342177280 | bytes 8388608 | tf_op jit(solution)/shard_map/middle/pallas_call | solution.py:455
  70.6 3.0 %last.1 = (f32[2,5,128,128]{3,2,1,0:T(8,128)S(1)}, f32[2,8,128]{2,1,0:T(8,128)S(1)}, f32[2,8,128]{2,1,0:T(8,128)S(1)}, bf16[1376,128]{1,0:T(8,128)(2,1)S(1)}, bf...) custom-call(s32[72]{0:T(128)S(1)} %pad_add_fusion.meta, bf16[9,5,128,128]{3,2,1,0:T(8,128)(2,1)S(1)} %get-tuple-element.36.q_ref, ...), custom_call_target="tpu_custom_call" | custom-call | flops 671088640 | bytes 8388608 | tf_op jit(solution)/shard_map/last/pallas_call | solution.py:468
  73.6 0.1 collective-permute-start.18
  73.7 0.3 collective-permute-start.19
  74.0 1.5 collective-permute-start.20
  75.5 9.6 %collective-permute-done.19.r2 = bf16[1376,128]{1,0:T(8,128)(2,1)S(1)} collective-permute-done((bf16[1376,128]{1,0:T(8,128)(2,1)S(1)}, bf16[1376,128]{1,0:T(8,128)(2,1)S(1)}, u32[]{:S(2)}, u32[]{:S(2)}) %collective-permute-start.19) | collective-permute-done | bytes 352288 | tf_op jit(solution)/shard_map/ppermute | solution.py:489
  85.1 6.0 %collective-permute-done.20.r3 = bf16[1376,128]{1,0:T(8,128)(2,1)S(1)} collective-permute-done((bf16[1376,128]{1,0:T(8,128)(2,1)S(1)}, bf16[1376,128]{1,0:T(8,128)(2,1)S(1)}, u32[]{:S(2)}, u32[]{:S(2)}) %collective-permute-start.20) | collective-permute-done | bytes 352288 | tf_op jit(solution)/shard_map/ppermute | solution.py:489
  91.1 2.9 %copy-done = bf16[640,5120]{1,0:T(8,128)(2,1)S(1)} copy-done((bf16[640,5120]{1,0:T(8,128)(2,1)S(1)}, bf16[640,5120]{1,0:T(8,128)(2,1)}, u32[]{:S(2)}) %copy-start) | copy-done | bytes 6553624
  94.0 6.7 %combine.1 = (f32[256,640]{1,0:T(8,128)S(1)}, bf16[256,640]{1,0:T(8,128)(2,1)S(1)}, bf16[256,640]{1,0:T(8,128)(2,1)S(1)}, bf16[256,640]{1,0:T(8,128)(2,1)}, bf16...) custom-call(s32[72]{0:T(128)S(1)} %pad_add_fusion.meta, ...), custom_call_target="tpu_custom_call" | custom-call | flops 1677721600 | bytes 12582912 | tf_op jit(solution)/shard_map/combine/pallas_call | solution.py:494
  100.7 0.0 copy-start.5
  100.7 1.7 %collective-permute-start.21 = (bf16[256,640]{1,0:T(8,128)(2,1)S(1)}, bf16[256,640]{1,0:T(8,128)(2,1)S(1)}, u32[]{:S(2)}, u32[]{:S(2)}) collective-permute-start(bf16[256,640]{1,0:T(8,128)(2,1)S(1)} %get-tuple-element.53), channel_id=1, source_target_pairs={{0,1},{1,0},{2,3},{3,2},{4,5},{5,4},{6,7},{7,6},{8,9},{9,8},{10,11... | collective-permute-start | bytes 983048 | tf_op jit(solution)/shard_map/ppermute | solution.py:517
  102.3 2.9 %collective-permute-start.22 = (bf16[256,640]{1,0:T(8,128)(2,1)S(1)}, bf16[256,640]{1,0:T(8,128)(2,1)S(1)}, u32[]{:S(2)}, u32[]{:S(2)}) collective-permute-start(bf16[256,640]{1,0:T(8,128)(2,1)S(1)} %get-tuple-element.54), channel_id=1, source_target_pairs={{0,2},{1,3},{2,0},{3,1},{4,6},{5,7},{6,4},{7,5},{8,10},{9,11},{10,... | collective-permute-start | bytes 983048 | tf_op jit(solution)/shard_map/ppermute | solution.py:517
  105.2 0.2 collective-permute-start.23
  105.5 2.4 %collective-permute-start.24 = (bf16[256,640]{1,0:T(8,128)(2,1)}, bf16[256,640]{1,0:T(8,128)(2,1)S(1)}, u32[]{:S(2)}, u32[]{:S(2)}) collective-permute-start(bf16[256,640]{1,0:T(8,128)(2,1)} %get-tuple-element.56), channel_id=1, source_target_pairs={{0,4},{1,5},{2,6},{3,7},{4,0},{5,1},{6,2},{7,3},{8,12},{9,13},{10,... | collective-permute-start | bytes 983048 | tf_op jit(solution)/shard_map/ppermute | solution.py:517
  107.9 0.9 collective-permute-start.25
  108.8 2.5 %collective-permute-done.21 = bf16[256,640]{1,0:T(8,128)(2,1)S(1)} collective-permute-done((bf16[256,640]{1,0:T(8,128)(2,1)S(1)}, bf16[256,640]{1,0:T(8,128)(2,1)S(1)}, u32[]{:S(2)}, u32[]{:S(2)}) %collective-permute-start.21) | collective-permute-done | bytes 327712 | tf_op jit(solution)/shard_map/ppermute | solution.py:517
  111.3 5.0 %collective-permute-start.26 = (bf16[256,640]{1,0:T(8,128)(2,1)S(1)}, bf16[256,640]{1,0:T(8,128)(2,1)}, u32[]{:S(2)}, u32[]{:S(2)}) collective-permute-start(bf16[256,640]{1,0:T(8,128)(2,1)S(1)} %get-tuple-element.58), channel_id=1, source_target_pairs={{0,6},{1,7},{2,4},{3,5},{4,2},{5,3},{6,0},{7,1},{8,14},{9,15},{10,... | collective-permute-start | bytes 983048 | tf_op jit(solution)/shard_map/ppermute | solution.py:517
  116.4 18.2 %collective-permute-done.22 = bf16[256,640]{1,0:T(8,128)(2,1)S(1)} collective-permute-done((bf16[256,640]{1,0:T(8,128)(2,1)S(1)}, bf16[256,640]{1,0:T(8,128)(2,1)S(1)}, u32[]{:S(2)}, u32[]{:S(2)}) %collective-permute-start.22) | collective-permute-done | bytes 327712 | tf_op jit(solution)/shard_map/ppermute | solution.py:517
  134.5 2.1 %collective-permute-start.27 = (bf16[256,640]{1,0:T(8,128)(2,1)S(1)}, bf16[256,640]{1,0:T(8,128)(2,1)}, u32[]{:S(2)}, u32[]{:S(2)}) collective-permute-start(bf16[256,640]{1,0:T(8,128)(2,1)S(1)} %get-tuple-element.59), channel_id=1, source_target_pairs={{0,7},{1,6},{2,5},{3,4},{4,3},{5,2},{6,1},{7,0},{8,15},{9,14},{10,... | collective-permute-start | bytes 983048 | tf_op jit(solution)/shard_map/ppermute | solution.py:517
  136.6 11.0 %collective-permute-done.27 = bf16[256,640]{1,0:T(8,128)(2,1)} collective-permute-done((bf16[256,640]{1,0:T(8,128)(2,1)S(1)}, bf16[256,640]{1,0:T(8,128)(2,1)}, u32[]{:S(2)}, u32[]{:S(2)}) %collective-permute-start.27) | collective-permute-done | bytes 327712 | tf_op jit(solution)/shard_map/ppermute | solution.py:517
  147.6 1.6 %fusion = (f32[256]{0:T(256)S(1)}, bf16[256,640]{1,0:T(8,128)(2,1)S(1)}) fusion(bf16[256,640]{1,0:T(8,128)(2,1)} %collective-permute-done.27, bf16[256,640]{1,0:T(8,128)(2,1)} %collective-permute-done.26, bf16[256,640]{1,0:T(8,128)(2,1)S(1)} %collective-permute-done.25, bf16[256,640]{1,0:T(8,128)(2,1)S(1)} %collective-permute-done.24, ...), kind=kLoop, calls=%fused_computation.2 | loop fusion | flops 3276544 | bytes 3605508 | tf_op jit(solution)/shard_map/reduce_sum | solution.py:524
  149.3 0.7 broadcast_in_dim.88
  150.0 3.7 %all-to-all-start = ((f32[8,8,128]{2,1,0:T(8,128)}), f32[8,8,128]{2,1,0:T(8,128)S(1)}, u32[]{:S(2)}, u32[]{:S(2)}) async-start(f32[8,8,128]{2,1,0:T(8,128)} %broadcast_in_dim.88), calls=%async_computation | async-start | bytes 65536 | tf_op jit(solution)/shard_map/all_to_all | solution.py:526
  153.7 7.7 %all-to-all-done = f32[8,8,128]{2,1,0:T(8,128)S(1)} async-done(((f32[8,8,128]{2,1,0:T(8,128)}), f32[8,8,128]{2,1,0:T(8,128)S(1)}, u32[]{:S(2)}, u32[]{:S(2)}) %all-to-all-start) | async-done | bytes 32800 | tf_op jit(solution)/shard_map/all_to_all | solution.py:526
  161.4 0.9 fusion.2
  (37 shorter events, 0.2 us)
Async XLA Ops:
  0.6 36.6 %copy-start.1 = (bf16[256,640]{1,0:T(8,128)(2,1)S(1)}, bf16[256,640]{1,0:T(8,128)(2,1)}, u32[]{:S(2)}) copy-start(bf16[256,640]{1,0:T(8,128)(2,1)} %q_in.1) | copy-start | bytes 983044
  0.6 36.6 %copy-start.2 = (bf16[256,128]{1,0:T(8,128)(2,1)S(1)}, bf16[256,128]{1,0:T(8,128)(2,1)}, u32[]{:S(2)}) copy-start(bf16[256,128]{1,0:T(8,128)(2,1)} %k_in.1) | copy-start | bytes 196612
  0.7 36.6 %copy-start.3 = (bf16[256,128]{1,0:T(8,128)(2,1)S(1)}, bf16[256,128]{1,0:T(8,128)(2,1)}, u32[]{:S(2)}) copy-start(bf16[256,128]{1,0:T(8,128)(2,1)} %v_in.1) | copy-start | bytes 196612
  2.8 12.7 %collective-permute-start.4 = (bf16[2,512,128]{2,1,0:T(8,128)(2,1)S(1)}, bf16[2,512,128]{2,1,0:T(8,128)(2,1)S(1)}, u32[]{:S(2)}, u32[]{:S(2)}) collective-permute-start(bf16[2,512,128]{2,1,0:T(8,128)(2,1)S(1)} %get-tuple-element.68.rest_0_), channel_id=1, source_target_pairs={{0,32},{8,40},{16,48},{24,56},{32,64},{40,72},{48,80},{56,88},{64,... | collective-permute-start | bytes 786440 | tf_op jit(solution)/shard_map/ppermute | solution.py:358
  4.7 10.9 %collective-permute-start.5 = (bf16[2,512,128]{2,1,0:T(8,128)(2,1)S(1)}, bf16[2,512,128]{2,1,0:T(8,128)(2,1)S(1)}, u32[]{:S(2)}, u32[]{:S(2)}) collective-permute-start(bf16[2,512,128]{2,1,0:T(8,128)(2,1)S(1)} %get-tuple-element.68.rest_0_), channel_id=1, source_target_pairs={{0,224},{8,232},{16,240},{24,248},{32,0},{40,8},{48,16},{56,24},{6... | collective-permute-start | bytes 786440 | tf_op jit(solution)/shard_map/ppermute | solution.py:359
  8.8 16.1 %collective-permute-start = (bf16[256,640]{1,0:T(8,128)(2,1)}, bf16[256,640]{1,0:T(8,128)(2,1)S(1)}, u32[]{:S(2)}, u32[]{:S(2)}) collective-permute-start(bf16[256,640]{1,0:T(8,128)(2,1)} %q_in.1), channel_id=1, source_target_pairs={{0,8},{8,0},{16,24},{24,16},{32,40},{40,32},{48,56},{56,48},{64,72... | collective-permute-start | bytes 983048 | tf_op jit(solution)/shard_map/ppermute | solution.py:350
  8.8 17.5 %collective-permute-start.1 = (bf16[256,640]{1,0:T(8,128)(2,1)}, bf16[256,640]{1,0:T(8,128)(2,1)S(1)}, u32[]{:S(2)}, u32[]{:S(2)}) collective-permute-start(bf16[256,640]{1,0:T(8,128)(2,1)} %q_in.1), channel_id=1, source_target_pairs={{0,16},{8,24},{16,0},{24,8},{32,48},{40,56},{48,32},{56,40},{64,80... | collective-permute-start | bytes 983048 | tf_op jit(solution)/shard_map/ppermute | solution.py:350
  9.3 3.9 %collective-permute-start.3 = (bf16[2,512,128]{2,1,0:T(8,128)(2,1)S(1)}, bf16[2,512,128]{2,1,0:T(8,128)(2,1)S(1)}, u32[]{:S(2)}, u32[]{:S(2)}) collective-permute-start(bf16[2,512,128]{2,1,0:T(8,128)(2,1)S(1)} %get-tuple-element.67), channel_id=1, source_target_pairs={{0,8},{8,0},{16,24},{24,16},{32,40},{40,32},{48,56},{56,48},{64,72... | collective-permute-start | bytes 786440 | tf_op jit(solution)/shard_map/ppermute | solution.py:347
  13.2 8.5 %collective-permute-start.7 = (bf16[2,512,128]{2,1,0:T(8,128)(2,1)S(1)}, bf16[2,512,128]{2,1,0:T(8,128)(2,1)S(1)}, u32[]{:S(2)}, u32[]{:S(2)}) collective-permute-start(bf16[2,512,128]{2,1,0:T(8,128)(2,1)S(1)} %collective-permute-done.3.rest_1_), channel_id=1, source_target_pairs={{0,224},{8,232},{16,240},{24,248},{32,0},{40,8},{48,16},{56,24},{6... | collective-permute-start | bytes 786440 | tf_op jit(solution)/shard_map/ppermute | solution.py:359
  15.5 11.1 %collective-permute-start.6 = (bf16[2,512,128]{2,1,0:T(8,128)(2,1)S(1)}, bf16[2,512,128]{2,1,0:T(8,128)(2,1)S(1)}, u32[]{:S(2)}, u32[]{:S(2)}) collective-permute-start(bf16[2,512,128]{2,1,0:T(8,128)(2,1)S(1)} %collective-permute-done.3.rest_1_), channel_id=1, source_target_pairs={{0,32},{8,40},{16,48},{24,56},{32,64},{40,72},{48,80},{56,88},{64,... | collective-permute-start | bytes 786440 | tf_op jit(solution)/shard_map/ppermute | solution.py:358
  15.7 14.9 %collective-permute-start.8 = (bf16[2,512,128]{2,1,0:T(8,128)(2,1)S(1)}, bf16[2,512,128]{2,1,0:T(8,128)(2,1)S(1)}, u32[]{:S(2)}, u32[]{:S(2)}) collective-permute-start(bf16[2,512,128]{2,1,0:T(8,128)(2,1)S(1)} %collective-permute-done.4.rest_2_), channel_id=1, source_target_pairs={{0,32},{8,40},{16,48},{24,56},{32,64},{40,72},{48,80},{56,88},{64,... | collective-permute-start | bytes 786440 | tf_op jit(solution)/shard_map/ppermute | solution.py:358
  21.7 9.8 %collective-permute-start.11 = (bf16[2,512,128]{2,1,0:T(8,128)(2,1)S(1)}, bf16[2,512,128]{2,1,0:T(8,128)(2,1)S(1)}, u32[]{:S(2)}, u32[]{:S(2)}) collective-permute-start(bf16[2,512,128]{2,1,0:T(8,128)(2,1)S(1)} %collective-permute-done.7.rest_5_), channel_id=1, source_target_pairs={{0,224},{8,232},{16,240},{24,248},{32,0},{40,8},{48,16},{56,24},{6... | collective-permute-start | bytes 786440 | tf_op jit(solution)/shard_map/ppermute | solution.py:359
  24.9 21.6 %collective-permute-start.2 = (bf16[256,640]{1,0:T(8,128)(2,1)}, bf16[256,640]{1,0:T(8,128)(2,1)S(1)}, u32[]{:S(2)}, u32[]{:S(2)}) collective-permute-start(bf16[256,640]{1,0:T(8,128)(2,1)} %q_in.1), channel_id=1, source_target_pairs={{0,24},{8,16},{16,8},{24,0},{32,56},{40,48},{48,40},{56,32},{64,88... | collective-permute-start | bytes 983048 | tf_op jit(solution)/shard_map/ppermute | solution.py:350
  26.3 12.4 %collective-permute-start.9 = (bf16[2,512,128]{2,1,0:T(8,128)(2,1)S(1)}, bf16[2,512,128]{2,1,0:T(8,128)(2,1)S(1)}, u32[]{:S(2)}, u32[]{:S(2)}) collective-permute-start(bf16[2,512,128]{2,1,0:T(8,128)(2,1)S(1)} %collective-permute-done.5.rest_3_), channel_id=1, source_target_pairs={{0,224},{8,232},{16,240},{24,248},{32,0},{40,8},{48,16},{56,24},{6... | collective-permute-start | bytes 786440 | tf_op jit(solution)/shard_map/ppermute | solution.py:359
  26.6 14.3 %collective-permute-start.10 = (bf16[2,512,128]{2,1,0:T(8,128)(2,1)S(1)}, bf16[2,512,128]{2,1,0:T(8,128)(2,1)S(1)}, u32[]{:S(2)}, u32[]{:S(2)}) collective-permute-start(bf16[2,512,128]{2,1,0:T(8,128)(2,1)S(1)} %collective-permute-done.6.rest_4_), channel_id=1, source_target_pairs={{0,32},{8,40},{16,48},{24,56},{32,64},{40,72},{48,80},{56,88},{64,... | collective-permute-start | bytes 786440 | tf_op jit(solution)/shard_map/ppermute | solution.py:358
  30.6 11.8 %collective-permute-start.12 = (bf16[2,512,128]{2,1,0:T(8,128)(2,1)S(1)}, bf16[2,512,128]{2,1,0:T(8,128)(2,1)S(1)}, u32[]{:S(2)}, u32[]{:S(2)}) collective-permute-start(bf16[2,512,128]{2,1,0:T(8,128)(2,1)S(1)} %collective-permute-done.8.rest_0_), channel_id=1, source_target_pairs={{0,32},{8,40},{16,48},{24,56},{32,64},{40,72},{48,80},{56,88},{64,... | collective-permute-start | bytes 786440 | tf_op jit(solution)/shard_map/ppermute | solution.py:358
  31.5 11.5 %collective-permute-start.15 = (bf16[2,512,128]{2,1,0:T(8,128)(2,1)S(1)}, bf16[2,512,128]{2,1,0:T(8,128)(2,1)S(1)}, u32[]{:S(2)}, u32[]{:S(2)}) collective-permute-start(bf16[2,512,128]{2,1,0:T(8,128)(2,1)S(1)} %collective-permute-done.11.rest_3_), channel_id=1, source_target_pairs={{0,224},{8,232},{16,240},{24,248},{32,0},{40,8},{48,16},{56,24},{6... | collective-permute-start | bytes 786440 | tf_op jit(solution)/shard_map/ppermute | solution.py:359
  38.7 26.6 %collective-permute-start.13 = (bf16[2,512,128]{2,1,0:T(8,128)(2,1)S(1)}, bf16[2,512,128]{2,1,0:T(8,128)(2,1)S(1)}, u32[]{:S(2)}, u32[]{:S(2)}) collective-permute-start(bf16[2,512,128]{2,1,0:T(8,128)(2,1)S(1)} %collective-permute-done.9.rest_1_), channel_id=1, source_target_pairs={{0,224},{8,232},{16,240},{24,248},{32,0},{40,8},{48,16},{56,24},{6... | collective-permute-start | bytes 786440 | tf_op jit(solution)/shard_map/ppermute | solution.py:359
  40.8 24.5 %collective-permute-start.14 = (bf16[2,512,128]{2,1,0:T(8,128)(2,1)S(1)}, bf16[2,512,128]{2,1,0:T(8,128)(2,1)S(1)}, u32[]{:S(2)}, u32[]{:S(2)}) collective-permute-start(bf16[2,512,128]{2,1,0:T(8,128)(2,1)S(1)} %collective-permute-done.10.rest_2_), channel_id=1, source_target_pairs={{0,32},{8,40},{16,48},{24,56},{32,64},{40,72},{48,80},{56,88},{64,... | collective-permute-start | bytes 786440 | tf_op jit(solution)/shard_map/ppermute | solution.py:358
  42.4 28.2 %collective-permute-start.16 = (bf16[2,512,128]{2,1,0:T(8,128)(2,1)S(1)}, bf16[2,512,128]{2,1,0:T(8,128)(2,1)S(1)}, u32[]{:S(2)}, u32[]{:S(2)}) collective-permute-start(bf16[2,512,128]{2,1,0:T(8,128)(2,1)S(1)} %collective-permute-done.12.rest_0_), channel_id=1, source_target_pairs={{0,32},{8,40},{16,48},{24,56},{32,64},{40,72},{48,80},{56,88},{64,... | collective-permute-start | bytes 786440 | tf_op jit(solution)/shard_map/ppermute | solution.py:363
  43.0 27.6 %collective-permute-start.17 = (bf16[2,512,128]{2,1,0:T(8,128)(2,1)S(1)}, bf16[2,512,128]{2,1,0:T(8,128)(2,1)S(1)}, u32[]{:S(2)}, u32[]{:S(2)}) collective-permute-start(bf16[2,512,128]{2,1,0:T(8,128)(2,1)S(1)} %collective-permute-done.15.rest_3_), channel_id=1, source_target_pairs={{0,224},{8,232},{16,240},{24,248},{32,0},{40,8},{48,16},{56,24},{6... | collective-permute-start | bytes 786440 | tf_op jit(solution)/shard_map/ppermute | solution.py:365
  73.6 2.0 %collective-permute-start.18 = (bf16[1376,128]{1,0:T(8,128)(2,1)S(1)}, bf16[1376,128]{1,0:T(8,128)(2,1)S(1)}, u32[]{:S(2)}, u32[]{:S(2)}) collective-permute-start(bf16[1376,128]{1,0:T(8,128)(2,1)S(1)} %get-tuple-element.49), channel_id=1, source_target_pairs={{0,8},{8,0},{16,24},{24,16},{32,40},{40,32},{48,56},{56,48},{64,72... | collective-permute-start | bytes 1056776 | tf_op jit(solution)/shard_map/ppermute | solution.py:489
  73.7 11.4 %collective-permute-start.19 = (bf16[1376,128]{1,0:T(8,128)(2,1)S(1)}, bf16[1376,128]{1,0:T(8,128)(2,1)S(1)}, u32[]{:S(2)}, u32[]{:S(2)}) collective-permute-start(bf16[1376,128]{1,0:T(8,128)(2,1)S(1)} %get-tuple-element.50), channel_id=1, source_target_pairs={{0,16},{8,24},{16,0},{24,8},{32,48},{40,56},{48,32},{56,40},{64,80... | collective-permute-start | bytes 1056776 | tf_op jit(solution)/shard_map/ppermute | solution.py:489
  74.0 17.1 %collective-permute-start.20 = (bf16[1376,128]{1,0:T(8,128)(2,1)S(1)}, bf16[1376,128]{1,0:T(8,128)(2,1)S(1)}, u32[]{:S(2)}, u32[]{:S(2)}) collective-permute-start(bf16[1376,128]{1,0:T(8,128)(2,1)S(1)} %get-tuple-element.51), channel_id=1, source_target_pairs={{0,24},{8,16},{16,8},{24,0},{32,56},{40,48},{48,40},{56,32},{64,88... | collective-permute-start | bytes 1056776 | tf_op jit(solution)/shard_map/ppermute | solution.py:489
  91.1 2.9 %copy-start = (bf16[640,5120]{1,0:T(8,128)(2,1)S(1)}, bf16[640,5120]{1,0:T(8,128)(2,1)}, u32[]{:S(2)}) copy-start(bf16[640,5120]{1,0:T(8,128)(2,1)} %weight_in.1) | copy-start | bytes 19660804
  100.7 53.0 %copy-start.5 = (bf16[640]{0:T(1024)(128)(2,1)S(1)}, bf16[640]{0:T(1024)(128)(2,1)}, u32[]{:S(2)}) copy-start(bf16[640]{0:T(1024)(128)(2,1)} %param.21) | copy-start | bytes 3844
  100.7 10.7 %collective-permute-start.21 = (bf16[256,640]{1,0:T(8,128)(2,1)S(1)}, bf16[256,640]{1,0:T(8,128)(2,1)S(1)}, u32[]{:S(2)}, u32[]{:S(2)}) collective-permute-start(bf16[256,640]{1,0:T(8,128)(2,1)S(1)} %get-tuple-element.53), channel_id=1, source_target_pairs={{0,1},{1,0},{2,3},{3,2},{4,5},{5,4},{6,7},{7,6},{8,9},{9,8},{10,11... | collective-permute-start | bytes 983048 | tf_op jit(solution)/shard_map/ppermute | solution.py:517
  102.3 32.2 %collective-permute-start.22 = (bf16[256,640]{1,0:T(8,128)(2,1)S(1)}, bf16[256,640]{1,0:T(8,128)(2,1)S(1)}, u32[]{:S(2)}, u32[]{:S(2)}) collective-permute-start(bf16[256,640]{1,0:T(8,128)(2,1)S(1)} %get-tuple-element.54), channel_id=1, source_target_pairs={{0,2},{1,3},{2,0},{3,1},{4,6},{5,7},{6,4},{7,5},{8,10},{9,11},{10,... | collective-permute-start | bytes 983048 | tf_op jit(solution)/shard_map/ppermute | solution.py:517
  105.2 31.4 %collective-permute-start.23 = (bf16[256,640]{1,0:T(8,128)(2,1)}, bf16[256,640]{1,0:T(8,128)(2,1)S(1)}, u32[]{:S(2)}, u32[]{:S(2)}) collective-permute-start(bf16[256,640]{1,0:T(8,128)(2,1)} %get-tuple-element.55), channel_id=1, source_target_pairs={{0,3},{1,2},{2,1},{3,0},{4,7},{5,6},{6,5},{7,4},{8,11},{9,10},{10,... | collective-permute-start | bytes 983048 | tf_op jit(solution)/shard_map/ppermute | solution.py:517
  105.5 31.2 %collective-permute-start.24 = (bf16[256,640]{1,0:T(8,128)(2,1)}, bf16[256,640]{1,0:T(8,128)(2,1)S(1)}, u32[]{:S(2)}, u32[]{:S(2)}) collective-permute-start(bf16[256,640]{1,0:T(8,128)(2,1)} %get-tuple-element.56), channel_id=1, source_target_pairs={{0,4},{1,5},{2,6},{3,7},{4,0},{5,1},{6,2},{7,3},{8,12},{9,13},{10,... | collective-permute-start | bytes 983048 | tf_op jit(solution)/shard_map/ppermute | solution.py:517
  107.9 28.8 %collective-permute-start.25 = (bf16[256,640]{1,0:T(8,128)(2,1)S(1)}, bf16[256,640]{1,0:T(8,128)(2,1)S(1)}, u32[]{:S(2)}, u32[]{:S(2)}) collective-permute-start(bf16[256,640]{1,0:T(8,128)(2,1)S(1)} %get-tuple-element.57), channel_id=1, source_target_pairs={{0,5},{1,4},{2,7},{3,6},{4,1},{5,0},{6,3},{7,2},{8,13},{9,12},{10,... | collective-permute-start | bytes 983048 | tf_op jit(solution)/shard_map/ppermute | solution.py:517
  111.3 25.3 %collective-permute-start.26 = (bf16[256,640]{1,0:T(8,128)(2,1)S(1)}, bf16[256,640]{1,0:T(8,128)(2,1)}, u32[]{:S(2)}, u32[]{:S(2)}) collective-permute-start(bf16[256,640]{1,0:T(8,128)(2,1)S(1)} %get-tuple-element.58), channel_id=1, source_target_pairs={{0,6},{1,7},{2,4},{3,5},{4,2},{5,3},{6,0},{7,1},{8,14},{9,15},{10,... | collective-permute-start | bytes 983048 | tf_op jit(solution)/shard_map/ppermute | solution.py:517
  134.5 13.1 %collective-permute-start.27 = (bf16[256,640]{1,0:T(8,128)(2,1)S(1)}, bf16[256,640]{1,0:T(8,128)(2,1)}, u32[]{:S(2)}, u32[]{:S(2)}) collective-permute-start(bf16[256,640]{1,0:T(8,128)(2,1)S(1)} %get-tuple-element.59), channel_id=1, source_target_pairs={{0,7},{1,6},{2,5},{3,4},{4,3},{5,2},{6,1},{7,0},{8,15},{9,14},{10,... | collective-permute-start | bytes 983048 | tf_op jit(solution)/shard_map/ppermute | solution.py:517
  149.3 13.1 %copy-start.4 = (bf16[256,640]{1,0:T(8,128)(2,1)}, bf16[256,640]{1,0:T(8,128)(2,1)S(1)}, u32[]{:S(2)}) copy-start(bf16[256,640]{1,0:T(8,128)(2,1)S(1)} %get-tuple-element.66) | copy-start | bytes 983044
  150.0 11.5 %all-to-all-start = ((f32[8,8,128]{2,1,0:T(8,128)}), f32[8,8,128]{2,1,0:T(8,128)S(1)}, u32[]{:S(2)}, u32[]{:S(2)}) async-start(f32[8,8,128]{2,1,0:T(8,128)} %broadcast_in_dim.88), calls=%async_computation | async-start | bytes 65536 | tf_op jit(solution)/shard_map/all_to_all | solution.py:526
